TPU v7x, 512 devices: a whole 4x4x16 slice. The times are simulated.
512 devices in a mesh: row: 16 (over z), wide: 32 (over x, y, core).
Axes of the slice: x: 4, y: 4, z: 16, core: 2. Of those that a mesh axis runs over, the one named last changes fastest.
Arguments:
- eigvec_t: float32 [2048, 32768], P(('row', 'wide')), may hold values from -6 to 6
- householder: float32 [64, 32, 32768], P('row', None, 'wide'), may hold values from -0.0625 to 0.0625
- wy_factor: float32 [6, 32, 32], replicated, may hold values from -0.5 to 0.5, as said below
- block_place: int32 [6], replicated, may hold values from 0 to 63, as said below
- offsets: int32 [6], replicated, may hold values from 0 to 16383, as said below
Outputs:
- vectors: float32 [2048, 32768], P('row', 'wide')
Inputs may be any that keep to these rules, and one draw needn't show every extreme that they name: wy_factor[s] is upper triangular. `offsets`: some step has offset 0 and some step has offset 32768 // 2 - 1. `block_place`: no stack position appears twice; positions 0 and 63 both appear.
All inputs are finite; a program needn't handle non-finite values.
Results may differ from a plain program's by a relative error of at most 0.0003.
Values sent between devices are 32-bit elements; how exact they have to be, the bound alone decides.
A program may use at most 64 MiB of HBM per device.

v0:
```python
import jax
import jax.numpy as jnp
from jax import lax
from jax.sharding import PartitionSpec as P


def spread(array, axis, root):
    mine = lax.axis_index(axis) == root
    return lax.psum(jnp.where(mine, array, jnp.zeros_like(array)), axis)


def body(eigvec_t, householder, wy_factor, block_place, offsets):
    highest = lax.Precision.HIGHEST
    current = lax.all_to_all(eigvec_t, "wide", split_axis=1, concat_axis=0, tiled=True)
    slots = householder.shape[0]
    ncols = current.shape[1]
    columns = lax.axis_index("wide") * ncols + jnp.arange(ncols, dtype=jnp.int32)
    steps = block_place.shape[0]

    def fetch_block(s):
        place = block_place[s]
        stored = lax.dynamic_index_in_dim(householder, place % slots, 0, keepdims=False)
        vecs = spread(stored, "row", place // slots)
        return jnp.where(columns[None, :] >= offsets[s], vecs, jnp.zeros_like(vecs))

    def factor_of(s):
        return lax.dynamic_index_in_dim(wy_factor, s, 0, keepdims=False)

    def single_turn(turn, state):
        for offset_in_turn in range(2):
            step_now = 2 * turn + offset_in_turn
            vecs = fetch_block(step_now)
            inner = lax.psum(jnp.dot(state, vecs.T, precision=highest), "wide")
            scaled = jnp.dot(inner, factor_of(step_now).T, precision=highest)
            state = state - jnp.dot(scaled, vecs, precision=highest)
        return state

    result = lax.fori_loop(0, steps // 2, single_turn, current)
    return result


def solution(mesh):
    return jax.shard_map(
        body,
        mesh=mesh,
        in_specs=(P(("row", "wide"), None), P("row", None, "wide"), P(), P(), P()),
        out_specs=P("row", "wide"),
        check_vma=False,
    )
```

profile of v0, /device:TPU:1, one launch (start us, length us, event | category | flops | bytes accessed | tf_op | source)
XLA Modules:
  0.0 1202.3 jit_solution(7988771504585214193)
XLA Ops:
  6.5 10.4 all-to-all-start
  17.0 11.7 all-to-all-done
  28.7 0.2 all_to_all.17
  28.9 0.9 copy-done.3
  29.7 0.0 copy-done.4
  29.7 0.0 copy-done.5
  29.7 1165.2 %while.17 = (s32[]{:T(128)}, f32[128,1024]{1,0:T(8,128)S(1)}, s32[6]{0:T(128)S(1)}, s32[6]{0:T(128)S(1)}, f32[4,32,1024]{2,1,0:T(8,128)S(1)}, /*index=5*/f32[6,3...) while((s32[]{:T(128)}, f32[128,1024]{1,0:T(8,128)S(1)}, ...), condition=%wide.region_5.6_spmd.clone, body=%wide.region_0.5_spmd.clone.sunk | while | flops 205008960 | bytes 7052183 | solution.py:38
  29.7 0.0 all-reduce.5.cloned.1.call-start
  29.8 0.7 fusion.68
  35.8 0.7 select_bitcast_fusion.3
  36.5 0.0 all-reduce.5.cloned.1.call-update
  36.5 0.6 fusion.69
  37.2 0.6 fusion.70
  37.7 0.6 fusion.72
  38.3 123.1 %all-reduce.5.cloned.1.call-done = (f32[32,1024]{1,0:T(8,128)}, f32[32,1024]{1,0:T(8,128)}) async-done(((f32[32,1024]{1,0:T(8,128)}, f32[32,1024]{1,0:T(8,128)}), (f32[32,1024]{1,0:T(8,128)}, f32[32,1024]{1,0:T(8,128)})) %all-reduce.5.cloned.1.call-update) | async-done | bytes 262160 | tf_op jit(solution)/shard_map/while/body/eval_jaxpr/psum | solution.py:9
  161.4 1.5 convolution_bitcast_fusion.2
  162.9 0.0 copy-start.2
  162.9 128.2 %psum.66 = f32[128,32]{0,1:T(8,128)S(1)} all-reduce(f32[128,32]{0,1:T(8,128)S(1)} %convolution_bitcast_fusion.2), channel_id=1, replica_groups=mesh['row'=16,'wide'=32] {'wide'}, use_global_device_ids=true, to_apply=%region_2.2 | all-reduce | flops 4096 | bytes 32768 | tf_op jit(solution)/shard_map/while/body/eval_jaxpr/psum | solution.py:33
  291.2 1.0 fusion.71
  292.2 0.6 convolution_subtract_fusion.4
  292.8 0.3 copy-done.1
  293.1 0.6 fusion.73
  293.7 123.8 %psum.67 = f32[128,32]{1,0:T(8,128)S(1)} all-reduce(f32[128,32]{1,0:T(8,128)S(1)} %fusion.73), channel_id=1, replica_groups=mesh['row'=16,'wide'=32] {'wide'}, use_global_device_ids=true, to_apply=%region_4.4 | all-reduce | flops 4096 | bytes 32768 | tf_op jit(solution)/shard_map/while/body/eval_jaxpr/psum | solution.py:33
  417.5 0.9 fusion.74
  418.4 0.6 convolution_subtract_fusion.5
  419.0 0.0 all-reduce.5.cloned.1.call-start
  419.0 0.7 fusion.68
  425.1 0.7 select_bitcast_fusion.3
  425.8 0.0 all-reduce.5.cloned.1.call-update
  425.8 0.6 fusion.69
  426.4 0.6 fusion.70
  427.0 0.6 fusion.72
  427.6 121.8 %all-reduce.5.cloned.1.call-done = (f32[32,1024]{1,0:T(8,128)}, f32[32,1024]{1,0:T(8,128)}) async-done(((f32[32,1024]{1,0:T(8,128)}, f32[32,1024]{1,0:T(8,128)}), (f32[32,1024]{1,0:T(8,128)}, f32[32,1024]{1,0:T(8,128)})) %all-reduce.5.cloned.1.call-update) | async-done | bytes 262160 | tf_op jit(solution)/shard_map/while/body/eval_jaxpr/psum | solution.py:9
  549.4 1.5 convolution_bitcast_fusion.2
  550.9 128.2 %psum.66 = f32[128,32]{0,1:T(8,128)S(1)} all-reduce(f32[128,32]{0,1:T(8,128)S(1)} %convolution_bitcast_fusion.2), channel_id=1, replica_groups=mesh['row'=16,'wide'=32] {'wide'}, use_global_device_ids=true, to_apply=%region_2.2 | all-reduce | flops 4096 | bytes 32768 | tf_op jit(solution)/shard_map/while/body/eval_jaxpr/psum | solution.py:33
  679.2 1.0 fusion.71
  680.2 0.6 convolution_subtract_fusion.4
  680.8 0.3 copy-done.1
  681.1 0.6 fusion.73
  681.6 123.8 %psum.67 = f32[128,32]{1,0:T(8,128)S(1)} all-reduce(f32[128,32]{1,0:T(8,128)S(1)} %fusion.73), channel_id=1, replica_groups=mesh['row'=16,'wide'=32] {'wide'}, use_global_device_ids=true, to_apply=%region_4.4 | all-reduce | flops 4096 | bytes 32768 | tf_op jit(solution)/shard_map/while/body/eval_jaxpr/psum | solution.py:33
  805.4 0.9 fusion.74
  806.4 0.6 convolution_subtract_fusion.5
  806.9 0.0 all-reduce.5.cloned.1.call-start
  807.0 0.7 fusion.68
  813.0 0.7 select_bitcast_fusion.3
  813.7 0.0 all-reduce.5.cloned.1.call-update
  813.8 0.6 fusion.69
  814.4 0.6 fusion.70
  815.0 0.6 fusion.72
  815.6 121.8 %all-reduce.5.cloned.1.call-done = (f32[32,1024]{1,0:T(8,128)}, f32[32,1024]{1,0:T(8,128)}) async-done(((f32[32,1024]{1,0:T(8,128)}, f32[32,1024]{1,0:T(8,128)}), (f32[32,1024]{1,0:T(8,128)}, f32[32,1024]{1,0:T(8,128)})) %all-reduce.5.cloned.1.call-update) | async-done | bytes 262160 | tf_op jit(solution)/shard_map/while/body/eval_jaxpr/psum | solution.py:9
  937.4 1.5 convolution_bitcast_fusion.2
  938.9 0.0 copy-start.2
  938.9 128.2 %psum.66 = f32[128,32]{0,1:T(8,128)S(1)} all-reduce(f32[128,32]{0,1:T(8,128)S(1)} %convolution_bitcast_fusion.2), channel_id=1, replica_groups=mesh['row'=16,'wide'=32] {'wide'}, use_global_device_ids=true, to_apply=%region_2.2 | all-reduce | flops 4096 | bytes 32768 | tf_op jit(solution)/shard_map/while/body/eval_jaxpr/psum | solution.py:33
  1067.1 1.0 fusion.71
  1068.2 0.0 copy-done.2
  1068.2 0.0 copy-start.1
  1068.2 0.6 convolution_subtract_fusion.4
  1068.8 0.3 copy-done.1
  1069.1 0.6 fusion.73
  1069.6 123.8 %psum.67 = f32[128,32]{1,0:T(8,128)S(1)} all-reduce(f32[128,32]{1,0:T(8,128)S(1)} %fusion.73), channel_id=1, replica_groups=mesh['row'=16,'wide'=32] {'wide'}, use_global_device_ids=true, to_apply=%region_4.4 | all-reduce | flops 4096 | bytes 32768 | tf_op jit(solution)/shard_map/while/body/eval_jaxpr/psum | solution.py:33
  1193.4 0.9 fusion.74
  1194.3 0.6 convolution_subtract_fusion.5
  1194.9 0.0 copy-start
  1194.9 0.8 copy-done
  (8 shorter events, 0.0 us)
Async XLA Ops:
  6.5 22.2 %all-to-all-start = ((f32[4,32,1024]{2,0,1:T(4,128)}), f32[4,32,1024]{2,0,1:T(4,128)S(1)}, u32[]{:S(2)}, u32[]{:S(2)}) async-start(f32[4,32,1024]{2,0,1:T(4,128)} %bitcast.53), calls=%async_computation | async-start | bytes 1048576 | tf_op jit(solution)/shard_map/all_to_all | solution.py:14
  28.7 1.0 copy-start.3
  28.7 1.0 copy-start.4
  28.7 1.0 copy-start.5
  29.7 131.7 %all-reduce.5.cloned.1.call-start = ((), (), s32[]{:S(2)}) async-start(), calls=%async_computation.1 | async-start | bytes 524288 | tf_op jit(solution)/shard_map/while/body/eval_jaxpr/psum | solution.py:9
  162.9 129.2 %copy-start.2 = (f32[32,1024]{1,0:T(8,128)S(1)}, f32[32,1024]{1,0:T(8,128)}, u32[]{:S(2)}) copy-start(f32[32,1024]{1,0:T(8,128)} %get-tuple-element.308) | copy-start | bytes 393220 | tf_op jit(solution)/shard_map/while
  292.2 0.9 copy-start.1
  419.0 130.4 %all-reduce.5.cloned.1.call-start = ((), (), s32[]{:S(2)}) async-start(), calls=%async_computation.1 | async-start | bytes 524288 | tf_op jit(solution)/shard_map/while/body/eval_jaxpr/psum | solution.py:9
  550.9 129.2 %copy-start.2 = (f32[32,1024]{1,0:T(8,128)S(1)}, f32[32,1024]{1,0:T(8,128)}, u32[]{:S(2)}) copy-start(f32[32,1024]{1,0:T(8,128)} %get-tuple-element.308) | copy-start | bytes 393220 | tf_op jit(solution)/shard_map/while
  680.2 0.9 copy-start.1
  806.9 130.4 %all-reduce.5.cloned.1.call-start = ((), (), s32[]{:S(2)}) async-start(), calls=%async_computation.1 | async-start | bytes 524288 | tf_op jit(solution)/shard_map/while/body/eval_jaxpr/psum | solution.py:9
  938.9 129.2 %copy-start.2 = (f32[32,1024]{1,0:T(8,128)S(1)}, f32[32,1024]{1,0:T(8,128)}, u32[]{:S(2)}) copy-start(f32[32,1024]{1,0:T(8,128)} %get-tuple-element.308) | copy-start | bytes 393220 | tf_op jit(solution)/shard_map/while
  1068.2 0.9 copy-start.1
  1194.9 0.8 copy-start
Sparse Core Ops, SparseCore 0:
  36.7 124.7 all-reduce.4
  425.9 123.4 all-reduce.4
  813.9 123.4 all-reduce.4
where the time goes:
time: 1210 us; the launch traced here: 1200 us
  blocking collectives  756 us (62%)
  waiting for transfers between devices  378 us (31%)
  loops' own time  16.5 us (1%)
  matrix products  15.4 us (1%)
  between operations  13.1 us (1%)
    psum x6, blocking collectives, single_turn(): inner = lax.psum(jnp.dot(state, vecs.T, precision=highest), 'wide')  756 us
    psum x3, waiting for transfers between devices, spread(): return lax.psum(jnp.where(mine, array, jnp.zeros_like(array)), axis)  367 us
  transfers between devices with their start and end apart: 4, of which 4 were waited for; matrix products, arithmetic and copies ran while one was open for 0% of the time, Pallas kernels for 0%

commit v1 on v0

v1 whole, which is shorter than its diff:
```python
import jax
import jax.numpy as jnp
from jax import lax
from jax.sharding import PartitionSpec as P

HIGHEST = lax.Precision.HIGHEST


def body(eigvec_t, householder, wy_factor, block_place, offsets):
    current = lax.all_to_all(eigvec_t, "wide", split_axis=1, concat_axis=0, tiled=True)
    slots, width, ncols = householder.shape
    steps = block_place.shape[0]
    rows = current.shape[0]
    columns = lax.axis_index("wide") * ncols + jnp.arange(ncols, dtype=jnp.int32)

    stored = jnp.take(householder, block_place % slots, axis=0)
    mine = (block_place // slots == lax.axis_index("row"))[:, None, None]
    keep = mine & (columns[None, None, :] >= offsets[:, None, None])
    vecs = lax.psum(jnp.where(keep, stored, 0.0), "row")
    vecs = vecs.reshape(steps * width, ncols)

    left = jnp.concatenate([current, vecs], axis=0)
    products = lax.psum(jnp.dot(left, vecs.T, precision=HIGHEST), "wide")
    inner, gram = products[:rows], products[rows:]

    scaled = []
    for s in range(steps):
        at = slice(s * width, (s + 1) * width)
        w = inner[:, at]
        if s:
            w = w - jnp.dot(jnp.concatenate(scaled, axis=1), gram[: s * width, at], precision=HIGHEST)
        scaled.append(jnp.dot(w, wy_factor[s].T, precision=HIGHEST))
    return current - jnp.dot(jnp.concatenate(scaled, axis=1), vecs, precision=HIGHEST)


def solution(mesh):
    return jax.shard_map(
        body,
        mesh=mesh,
        in_specs=(P(("row", "wide"), None), P("row", None, "wide"), P(), P(), P()),
        out_specs=P("row", "wide"),
        check_vma=False,
    )
```

time: 1210 us -> 300 us (0.25)
  blocking collectives: 756 us -> 21.2 us
  waiting for transfers between devices: 378 us -> 249 us
  loops' own time: 16.5 us -> 0 us
    psum x6 -> x0, blocking collectives: 756 us -> none  [single_turn(): inner = lax.psum(jnp.dot(state, vecs.T, precision=highest), 'wide')]
    psum x3 -> x2, waiting for transfers between devices: 367 us -> 249 us  [the longest x1 138 us: body(): products = lax.psum(jnp.dot(left, vecs.T, precision=HIGHEST), 'wide')]
    all_to_all x0 -> x1, blocking collectives: none -> 21.2 us  [body(): lax.all_to_all(eigvec_t, 'wide', split_axis=1, concat_axis=0, tiled=True)]
    another operation x1 -> x0, loops' own time: 16.5 us -> none  [body(): result = lax.fori_loop(0, steps // 2, single_turn, current)]
  transfers between devices with their start and end apart: 4 -> 2, of which waited for: 4 -> 2; matrix products, arithmetic and copies ran while one was open for 0% -> 0% of each run, Pallas kernels for 0% -> 0%
where the time goes in v1:
time: 300 us; the launch traced here: 299 us
  waiting for transfers between devices  249 us (83%)
  blocking collectives  21.2 us (7%)
  between operations  13.5 us (4%)
  matrix products  11.4 us (4%)
    psum x1, waiting for transfers between devices, body(): products = lax.psum(jnp.dot(left, vecs.T, precision=HIGHEST), 'wide')  138 us
    psum x1, waiting for transfers between devices, body(): vecs = lax.psum(jnp.where(keep, stored, 0.0), 'row')  112 us
    all_to_all x1, blocking collectives, body(): lax.all_to_all(eigvec_t, 'wide', split_axis=1, concat_axis=0, tiled=True)  21.2 us
  transfers between devices with their start and end apart: 2, of which 2 were waited for; matrix products, arithmetic and copies ran while one was open for 0% of the time, Pallas kernels for 0%

profile of v1, /device:TPU:1, one launch (start us, length us, event | category | flops | bytes accessed | tf_op | source)
XLA Modules:
  0.0 299.3 jit_solution(9482833532118108873)
XLA Ops:
  6.5 0.0 copy-start
  6.5 0.0 all-reduce.3.cloned.1.call-start
  6.5 0.7 compare_and_fusion.1
  7.3 0.3 copy-done
  7.6 0.0 copy-start.4
  7.6 0.6 gather_fusion
  8.2 0.0 copy-done.4
  8.2 0.1 compare_and_fusion
  8.3 1.1 select_select_fusion
  9.4 0.0 copy-start.2
  9.4 0.0 all-reduce.3.cloned.1.call-update
  9.4 0.0 all-reduce.5.cloned.1.call-start
  9.5 1.0 copy-done.2
  10.4 21.2 %all_to_all.19 = f32[4,32,1024]{2,0,1:T(4,128)S(1)} all-to-all(f32[4,32,1024]{2,0,1:T(4,128)S(1)} %bitcast.43), channel_id=1, replica_groups=mesh['row'=16,'wide'=32] {'wide'}, dimensions={1} | all-to-all | bytes 1048576 | tf_op jit(solution)/shard_map/all_to_all | solution.py:10
  31.7 0.2 all_to_all.17
  31.9 0.0 copy-start.3
  31.9 111.6 %all-reduce.3.cloned.1.call-done = f32[192,1024]{1,0:T(8,128)} async-done(((f32[192,1024]{1,0:T(8,128)}), f32[192,1024]{1,0:T(8,128)}) %all-reduce.3.cloned.1.call-update) | async-done | bytes 786448 | tf_op jit(solution)/shard_map/psum | solution.py:19
  143.5 3.8 %fusion = f32[320,192]{0,1:T(8,128)} fusion(f32[192,1024]{1,0:T(8,128)} %all-reduce.3.cloned.1.call-done, f32[128,1024]{1,0:T(8,128)S(1)} %all_to_all.17), kind=kOutput, calls=%fused_computation.1 | convolution fusion | flops 755302400 | bytes 1556480 | tf_op jit(solution)/shard_map/dot_general | solution.py:23
  147.3 0.0 copy-start.1
  147.3 0.0 all-reduce.5.cloned.1.call-update
  147.3 137.5 %all-reduce.5.cloned.1.call-done = f32[320,192]{0,1:T(8,128)} async-done(((f32[320,192]{0,1:T(8,128)}), f32[320,192]{0,1:T(8,128)}) %all-reduce.5.cloned.1.call-update) | async-done | bytes 245776 | tf_op jit(solution)/shard_map/psum | solution.py:23
  284.9 0.0 copy-done.3
  284.9 0.9 constant_dynamic-update-slice_fusion.4
  285.7 0.9 convolution_subtract_fusion.5
  286.6 0.1 constant_dynamic-update-slice_fusion.3
  286.7 0.9 convolution_subtract_fusion.4
  287.6 0.1 constant_dynamic-update-slice_fusion.2
  287.8 0.9 convolution_subtract_fusion.3
  288.7 0.1 constant_dynamic-update-slice_fusion.1
  288.8 0.9 convolution_subtract_fusion.2
  289.8 0.1 constant_dynamic-update-slice_fusion
  289.9 1.0 convolution_subtract_fusion.1
  290.9 0.1 convolution_dynamic-update-slice_fusion
  291.0 0.0 copy-done.1
  291.0 1.5 convolution_subtract_fusion
  (2 shorter events, 0.0 us)
Async XLA Ops:
  6.5 1.1 copy-start
  6.5 136.9 %all-reduce.3.cloned.1.call-start = ((), (), s32[]{:S(2)}) async-start(), calls=%async_computation.1 | async-start | bytes 1572864 | tf_op jit(solution)/shard_map/psum | solution.py:19
  7.6 0.7 copy-start.4
  9.4 1.0 copy-start.2
  9.4 275.4 %all-reduce.5.cloned.1.call-start = ((), (), s32[]{:S(2)}) async-start(), calls=%async_computation.2 | async-start | bytes 589824 | tf_op jit(solution)/shard_map/psum | solution.py:23
  31.9 253.0 %copy-start.3 = (f32[6,32,32]{2,1,0:T(8,128)S(1)}, f32[6,32,32]{2,1,0:T(8,128)}, u32[]{:S(2)}) copy-start(f32[6,32,32]{2,1,0:T(8,128)} %param.7) | copy-start | bytes 73732
  147.3 143.7 %copy-start.1 = (f32[192,1024]{1,0:T(8,128)S(1)}, f32[192,1024]{1,0:T(8,128)}, u32[]{:S(2)}) copy-start(f32[192,1024]{1,0:T(8,128)} %all-reduce.3.cloned.1.call-done) | copy-start | bytes 2359300
Sparse Core Ops, SparseCore 0:
  9.7 133.7 all-reduce.2
  147.4 137.3 all-reduce.4

commit v2 on v1

v2 whole, which is shorter than its diff:
```python
import functools

import jax
import jax.numpy as jnp
from jax import lax
from jax.experimental import pallas as pl
from jax.experimental.pallas import tpu as pltpu
from jax.sharding import PartitionSpec as P

HIGHEST = lax.Precision.HIGHEST
MESH = pl.DeviceIdType.MESH
STEPS, BW, SLAB = 6, 32, 128
GRAM_TILES = [(i, 0) for i in range(12)] + [(i, 1) for i in range(20)]


def dot_t(a, b):
    return lax.dot_general(a, b, (((1,), (1,)), ((), ())), precision=HIGHEST, preferred_element_type=jnp.float32)


def dot(a, b):
    return jnp.dot(a, b, precision=HIGHEST, preferred_element_type=jnp.float32)


def kernel(n_row, n_wide, place_ref, offset_ref, x_ref, h_ref, t_ref, out_ref,
           own, right_buf, left_buf, xs, vs, part, gather_in, total, gathered,
           right_sem, left_sem, x_sem, red_sem, all_sem, send_sem, local_sem):
    r = lax.axis_index("row")
    w = lax.axis_index("wide")
    slots = h_ref.shape[0]
    slabs = h_ref.shape[2] // SLAB
    per = slabs * STEPS // n_row
    right = lax.rem(r + 1, n_row)
    left = lax.rem(r + n_row - 1, n_row)

    barrier = pltpu.get_barrier_semaphore()
    pl.semaphore_signal(barrier, inc=1, device_id={"row": right}, device_id_type=MESH)
    pl.semaphore_signal(barrier, inc=1, device_id={"row": left}, device_id_type=MESH)

    def greet(d, carry):
        peer = lax.rem(w + d, n_wide)
        pl.semaphore_signal(barrier, inc=1, device_id={"wide": peer}, device_id_type=MESH)
        return carry

    lax.fori_loop(1, n_wide, greet, 0)

    lane = lax.broadcasted_iota(jnp.int32, (BW, SLAB), 1) + w * (slabs * SLAB)
    for s in range(STEPS):
        place = place_ref[s]
        start = jnp.where(lax.div(place, slots) == r, offset_ref[s], n_wide * slabs * SLAB)
        slot = lax.rem(place, slots)
        for k in range(slabs):
            block = h_ref[slot, :, k * SLAB:(k + 1) * SLAB]
            own[k * STEPS + s] = jnp.where(lane + k * SLAB >= start, block, 0.0)

    mine = pltpu.make_async_copy(x_ref.at[w], xs.at[:, w], local_sem)
    mine.start()
    pl.semaphore_wait(barrier, n_wide + 1)

    def send_x(d):
        peer = lax.rem(w + d, n_wide)
        pltpu.make_async_remote_copy(
            src_ref=x_ref.at[peer], dst_ref=xs.at[:, w], send_sem=send_sem.at[2], recv_sem=x_sem,
            device_id={"wide": peer}, device_id_type=MESH).start()

    def hop(buf, c, sems, send, t, j, to):
        return pltpu.make_async_remote_copy(
            src_ref=buf.at[c], dst_ref=buf.at[c], send_sem=send, recv_sem=sems.at[(t + 1) * per + j],
            device_id={"row": to}, device_id_type=MESH)

    def step(t, first=False, last=False):
        c_right = lax.rem(r - t + n_row, n_row) * per
        c_left = lax.rem(r + 1 + t, n_row) * per
        for j in range(per):
            for buf, c, sems, send, to in ((right_buf, c_right + j, right_sem, send_sem.at[0], right),
                                           (left_buf, c_left + j, left_sem, send_sem.at[1], left)):
                if first:
                    buf[c] = own[c]
                else:
                    hop(buf, c, sems, send, t - 1, j, to).wait_recv()
                    buf[c] = buf[c] + own[c]
                if not last:
                    hop(buf, c, sems, send, t, j, to).start()

    step(0, first=True)
    send_x(1)

    def middle(t, carry):
        step(t)
        send_x(2 * t)
        send_x(2 * t + 1)
        return carry

    lax.fori_loop(1, n_row - 1, middle, 0)
    for d in range(2 * n_row - 2, n_wide):
        send_x(d)
    step(n_row - 1, last=True)

    def all_but_one(buf, send, recv, count):
        return pltpu.make_async_remote_copy(
            src_ref=buf.at[pl.ds(0, count)], dst_ref=buf.at[pl.ds(0, count)], send_sem=send, recv_sem=recv,
            device_id={"row": right}, device_id_type=MESH)

    mine.wait()
    x_rows = xs.shape[1] * xs.shape[2]
    other_x = pltpu.make_async_remote_copy(
        src_ref=x_ref.at[pl.ds(0, n_wide - 1)], dst_ref=xs.at[:, pl.ds(0, n_wide - 1)], send_sem=send_sem.at[2],
        recv_sem=x_sem, device_id={"row": right}, device_id_type=MESH)
    other_x.wait_recv()

    acc = None
    for k in range(slabs):
        at = slice(k * STEPS, (k + 1) * STEPS)
        v = (right_buf[at] + left_buf[at] - own[at]).reshape(STEPS * BW, SLAB)
        vs[k] = v
        x = xs[k].reshape(x_rows, SLAB)
        product = dot_t(jnp.concatenate([x, v], axis=0), v)
        acc = product if acc is None else acc + product

    wide = 2 * SLAB
    padded = jnp.concatenate([acc, jnp.zeros((acc.shape[0], wide - acc.shape[1]), jnp.float32)], axis=1)
    first_gram = x_rows // 8
    for peer in range(n_wide):
        i, c = peer // 2, peer % 2
        part[peer, 0] = padded[i * 8:(i + 1) * 8, c * SLAB:(c + 1) * SLAB]
        i, c = GRAM_TILES[peer]
        i = i + first_gram
        part[peer, 1] = padded[i * 8:(i + 1) * 8, c * SLAB:(c + 1) * SLAB]

    def scatter(d, carry):
        peer = lax.rem(w + d, n_wide)
        pltpu.make_async_remote_copy(
            src_ref=part.at[peer], dst_ref=gather_in.at[w], send_sem=send_sem.at[3], recv_sem=red_sem,
            device_id={"wide": peer}, device_id_type=MESH).start()
        return carry

    lax.fori_loop(1, n_wide, scatter, 0)
    gather_in[w] = part[w]
    all_but_one(gather_in, send_sem.at[3], red_sem, n_wide - 1).wait_recv()
    total[...] = jnp.sum(gather_in[...], axis=0)

    def share(d, carry):
        peer = lax.rem(w + d, n_wide)
        pltpu.make_async_remote_copy(
            src_ref=total, dst_ref=gathered.at[w], send_sem=send_sem.at[4], recv_sem=all_sem,
            device_id={"wide": peer}, device_id_type=MESH).start()
        return carry

    lax.fori_loop(1, n_wide, share, 0)
    gathered[w] = total[...]
    all_but_one(gathered, send_sem.at[4], all_sem, n_wide - 1).wait_recv()

    halves = [jnp.concatenate([gathered[2 * i + c, 0] for i in range(n_wide // 2)], axis=0) for c in range(2)]
    inner = jnp.concatenate(halves, axis=1)
    gram0 = jnp.concatenate([gathered[i, 1] for i in range(12)], axis=0)
    gram1 = jnp.concatenate([gathered[i, 1] for i in range(12, 32)], axis=0)
    scaled = []
    for s in range(STEPS):
        at = slice(s * BW, (s + 1) * BW)
        value = inner[:, at]
        gram, first = (gram0, 0) if s < 4 else (gram1, SLAB)
        if s:
            overlap = gram[:s * BW, s * BW - first:(s + 1) * BW - first]
            value = value - dot(jnp.concatenate(scaled, axis=1), overlap)
        scaled.append(dot_t(value, t_ref[s]))
    u = jnp.concatenate(scaled, axis=1)
    for k in range(slabs):
        out_ref[:, k * SLAB:(k + 1) * SLAB] = xs[k].reshape(x_rows, SLAB) - dot(u, vs[k])

    sent = (n_row - 1) * per
    all_but_one(right_buf, send_sem.at[0], right_sem.at[0], sent).wait_send()
    all_but_one(left_buf, send_sem.at[1], left_sem.at[0], sent).wait_send()
    other_x.wait_send()
    all_but_one(part, send_sem.at[3], red_sem, n_wide - 1).wait_send()
    all_but_one(gathered, send_sem.at[4], all_sem, n_wide - 1).wait_send()


def body(n_row, n_wide, eigvec_t, householder, wy_factor, block_place, offsets):
    local = eigvec_t.shape[0]
    ncols = householder.shape[2]
    slabs = ncols // SLAB
    x = eigvec_t.reshape(local, n_wide, slabs, SLAB).transpose(1, 2, 0, 3)
    chunks = slabs * STEPS
    vmem = pl.BlockSpec(memory_space=pltpu.VMEM)
    smem = pl.BlockSpec(memory_space=pltpu.SMEM)
    f32 = jnp.float32
    return pl.pallas_call(
        functools.partial(kernel, n_row, n_wide),
        out_shape=jax.ShapeDtypeStruct((local * n_wide, ncols), f32),
        in_specs=[smem, smem, pl.BlockSpec(memory_space=pl.ANY), vmem, vmem],
        out_specs=vmem,
        scratch_shapes=[
            pltpu.VMEM((chunks, BW, SLAB), f32),
            pltpu.VMEM((chunks, BW, SLAB), f32),
            pltpu.VMEM((chunks, BW, SLAB), f32),
            pltpu.VMEM((slabs, n_wide, local, SLAB), f32),
            pltpu.VMEM((slabs, STEPS * BW, SLAB), f32),
            pltpu.VMEM((n_wide, 2, 8, SLAB), f32),
            pltpu.VMEM((n_wide, 2, 8, SLAB), f32),
            pltpu.VMEM((2, 8, SLAB), f32),
            pltpu.VMEM((n_wide, 2, 8, SLAB), f32),
            pltpu.SemaphoreType.DMA((chunks,)),
            pltpu.SemaphoreType.DMA((chunks,)),
            pltpu.SemaphoreType.DMA,
            pltpu.SemaphoreType.DMA,
            pltpu.SemaphoreType.DMA,
            pltpu.SemaphoreType.DMA((5,)),
            pltpu.SemaphoreType.DMA,
        ],
        compiler_params=pltpu.CompilerParams(collective_id=0, has_side_effects=True, vmem_limit_bytes=32 << 20),
    )(block_place, offsets, x, householder, wy_factor)


def solution(mesh):
    n_row, n_wide = mesh.shape["row"], mesh.shape["wide"]
    return jax.shard_map(
        functools.partial(body, n_row, n_wide),
        mesh=mesh,
        in_specs=(P(("row", "wide"), None), P("row", None, "wide"), P(), P(), P()),
        out_specs=P("row", "wide"),
        check_vma=False,
    )
```

time: 300 us -> 90 us (0.30)
  waiting for transfers between devices: 249 us -> 0 us
  Pallas kernels: 0 us -> 85.3 us
  blocking collectives: 21.2 us -> 0 us
  between operations: 13.5 us -> 0.01 us
  matrix products: 11.4 us -> 0 us
    psum x2 -> x0, waiting for transfers between devices: 249 us -> none  [the longest x1 138 us: body(): products = lax.psum(jnp.dot(left, vecs.T, precision=HIGHEST), 'wide')]
    pallas_call x0 -> x1, Pallas kernels: none -> 85.3 us  [body(): pl.pallas_call(functools.partial(kernel, n_row, n_wide), out_shape=jax.Sh...]
    all_to_all x1 -> x0, blocking collectives: 21.2 us -> none  [body(): lax.all_to_all(eigvec_t, 'wide', split_axis=1, concat_axis=0, tiled=True)]
    dot_general x13 -> x0, matrix products: 11.4 us -> none  [the longest x5 4.56 us: body(): jnp.dot(jnp.concatenate(scaled, axis=1), gram[:s * width, at], precision=...]
    unnamed x10 -> x11, local copies, waits for them, and re-layouts: 1.34 us -> 4.44 us
  transfers between devices with their start and end apart: 2 -> 0, of which waited for: 2 -> 0; matrix products, arithmetic and copies ran while one was open for 0% -> 0% of each run, Pallas kernels for 0% -> 0%
where the time goes in v2:
time: 90 us; the launch traced here: 89.8 us
  Pallas kernels  85.3 us (95%)
  local copies, waits for them, and re-layouts  4.44 us (5%)
    pallas_call x1, Pallas kernels, body(): pl.pallas_call(functools.partial(kernel, n_row, n_wide), out_shape=jax.Sh...  85.3 us
    unnamed x11, local copies, waits for them, and re-layouts  4.44 us

profile of v2, /device:TPU:1, one launch (start us, length us, event | category | flops | bytes accessed | tf_op | source)
XLA Modules:
  0.0 89.8 jit_solution(15450393670446852739)
XLA Ops:
  0.0 0.0 copy-start.4
  0.0 0.0 copy-start.3
  0.0 0.7 copy-done.4
  0.7 0.0 copy-done.3
  0.7 0.0 copy-start
  0.7 1.0 %copy-done = f32[4,32768]{1,0:T(4,128)S(1)} copy-done((f32[4,32768]{1,0:T(4,128)S(1)}, f32[4,32768]{1,0:T(4,128)}, u32[]{:S(2)}) %copy-start) | copy-done | bytes 524312
  1.7 0.0 copy-start.1
  1.7 1.0 %copy-done.1 = f32[4,32,1024]{2,1,0:T(8,128)S(1)} copy-done((f32[4,32,1024]{2,1,0:T(8,128)S(1)}, f32[4,32,1024]{2,1,0:T(8,128)}, u32[]{:S(2)}) %copy-start.1) | copy-done | bytes 524312
  2.8 0.0 copy-start.2
  2.8 0.9 copy-done.2
  3.6 85.3 %shard_map.55 = f32[128,1024]{1,0:T(8,128)S(1)} custom-call(s32[6]{0:T(128)S(1)} %copy-done.3, s32[6]{0:T(128)S(1)} %copy-done.4, f32[32,8,4,128]{3,2,1,0:T(4,128)S(1)} %bitcast.3, f32[4,32,1024]{2,1,0:T(8,128)S(1)} %copy-done.1, f32[6,32,32]{2,1,0:T(8,128)S(1)} %copy-done.2), custom_call_target="tpu_custom_call" | custom-call | tf_op jit(solution)/shard_map/pallas_call | solution.py:186
  89.0 0.8 copy.7
Async XLA Ops:
  0.0 0.7 copy-start.4
  0.0 0.7 copy-start.3
  0.7 1.0 %copy-start = (f32[4,32768]{1,0:T(4,128)S(1)}, f32[4,32768]{1,0:T(4,128)}, u32[]{:S(2)}) copy-start(f32[4,32768]{1,0:T(4,128)} %param.5) | copy-start | bytes 1572868
  1.7 1.0 %copy-start.1 = (f32[4,32,1024]{2,1,0:T(8,128)S(1)}, f32[4,32,1024]{2,1,0:T(8,128)}, u32[]{:S(2)}) copy-start(f32[4,32,1024]{2,1,0:T(8,128)} %h_ref.1) | copy-start | bytes 1572868
  2.8 0.9 copy-start.2

commit v3 on v2

v3 whole, which is shorter than its diff:
```python
import functools

import jax
import jax.numpy as jnp
from jax import lax
from jax.experimental import pallas as pl
from jax.experimental.pallas import tpu as pltpu
from jax.sharding import PartitionSpec as P

HIGHEST = lax.Precision.HIGHEST
MESH = pl.DeviceIdType.MESH
STEPS, BW, SLAB, CUBE = 6, 32, 128, 4
HALF = STEPS // 2
GRAM_TILES = [(i, 0) for i in range(12)] + [(i, 1) for i in range(20)]


def dot_t(a, b):
    return lax.dot_general(a, b, (((1,), (1,)), ((), ())), precision=HIGHEST, preferred_element_type=jnp.float32)


def dot(a, b):
    return jnp.dot(a, b, precision=HIGHEST, preferred_element_type=jnp.float32)


def kernel(n_row, n_wide, place_ref, offset_ref, x_ref, h_hbm, t_hbm, out_ref,
           h_ref, t_ref, diag, own, feed, flow, vs, xs, part, gather_in, total, gathered,
           feed_sem, flow_sem, done_sem, x_sem, red_sem, all_sem, send_sem, local_sem):
    r = lax.axis_index("row")
    w = lax.axis_index("wide")
    slots = h_ref.shape[0]
    slabs = h_ref.shape[2] // SLAB
    pieces = slabs
    side = pieces * HALF
    q = lax.rem(r, 2)
    a = lax.div(r, 2)
    mine, other = q * side, (1 - q) * side

    def row(delta):
        return lax.rem(r + delta + n_row, n_row)

    near, far = row(1 - 2 * q), row(2 * q - 1)

    barrier = pltpu.get_barrier_semaphore()
    for delta in (1, -1, 2, -2):
        pl.semaphore_signal(barrier, inc=1, device_id={"row": row(delta)}, device_id_type=MESH)

    def greet(d, carry):
        peer = lax.rem(w + d, n_wide)
        pl.semaphore_signal(barrier, inc=1, device_id={"wide": peer}, device_id_type=MESH)
        return carry

    load_h = pltpu.make_async_copy(h_hbm, h_ref, local_sem.at[0])
    load_t = pltpu.make_async_copy(t_hbm, t_ref, local_sem.at[1])
    load_x = pltpu.make_async_copy(x_ref.at[w], xs.at[:, w], local_sem.at[2])
    load_h.start()
    load_t.start()
    load_x.start()
    lax.fori_loop(1, n_wide, greet, 0)
    load_h.wait()

    lane = lax.broadcasted_iota(jnp.int32, (BW, SLAB), 1) + w * (slabs * SLAB)
    for s in range(STEPS):
        place = place_ref[s]
        start = jnp.where(lax.div(place, slots) == r, offset_ref[s], n_wide * slabs * SLAB)
        slot = lax.rem(place, slots)
        for k in range(slabs):
            block = h_ref[slot, :, k * SLAB:(k + 1) * SLAB]
            own[(s // HALF) * side + k * HALF + s % HALF] = jnp.where(lane + k * SLAB >= start, block, 0.0)

    load_t.wait()
    diag[...] = jnp.zeros_like(diag)
    for s in range(STEPS):
        at = s * BW % SLAB
        diag[s * BW // SLAB, at:at + BW, at:at + BW] = t_ref[s]
    pl.semaphore_wait(barrier, n_wide + 3)

    def copy(src, dst, send, recv, to):
        return pltpu.make_async_remote_copy(
            src_ref=src, dst_ref=dst, send_sem=send, recv_sem=recv, device_id=to, device_id_type=MESH)

    def send_feed(i, to):
        for j in range(HALF):
            c = i * HALF + j
            copy(own.at[other + c], feed.at[c], send_sem.at[0], feed_sem.at[c], {"row": to}).start()

    for t in range(pieces // 2):
        i = lax.div(near, 2) - t + pieces
        send_feed(lax.rem(i + lax.rem(i, 2) * (1 + 2 * t), pieces), near)
        i = lax.div(far, 2) - t + pieces
        send_feed(lax.rem(i + (1 - lax.rem(i, 2)) * (1 + 2 * t), pieces), far)

    def send_x(d):
        peer = lax.rem(w + d, n_wide)
        copy(x_ref.at[peer], xs.at[:, w], send_sem.at[2], x_sem, {"wide": peer}).start()

    def hop(t, d, c, j):
        to = row(2 - 4 * d)
        return copy(flow.at[d, c], flow.at[d, c], send_sem.at[1], flow_sem.at[d, (t + 1) * HALF + j], {"row": to})

    def finished(i, c):
        sub = lax.rem(i, 2)
        to = near + sub * (far - near)
        return copy(vs.at[mine + c], vs.at[mine + c], send_sem.at[5], done_sem, {"row": to})

    def advance(t, d, early, first=False, last=False):
        i = lax.rem(a - t + d * (1 + 2 * t) + pieces, pieces)
        for j in range(HALF):
            c = i * HALF + j
            if early:
                copy(own.at[mine + c], feed.at[c], send_sem.at[0], feed_sem.at[c], {"row": near}).wait_recv()
                base = own[mine + c] + feed[c]
                own[mine + c] = base
            else:
                base = own[mine + c]
            if first:
                value = base
            else:
                hop(t - 1, d, c, j).wait_recv()
                value = flow[d, c] + base
            flow[d, c] = value
            if not last:
                hop(t, d, c, j).start()
            if not early:
                vs[mine + c] = value + flow[1 - d, c] - base
                finished(i, c).start()

    def both(t, early, last=False):
        crossed_right = lax.div(r + 2 * n_row, CUBE) - lax.div(r + 2 * n_row - 2 * t, CUBE)
        crossed_left = lax.div(r + 2 * t, CUBE) - lax.div(r, CUBE)
        d = lax.div(crossed_right - crossed_left + 1, 2)
        advance(t, d, early, last=last)
        advance(t, 1 - d, early, last=last)

    def spread(t, carry):
        share = n_wide * 2 // pieces
        lax.fori_loop(t * share, (t + 1) * share, lambda d, c: (send_x(d), c)[1], 0)
        return carry

    advance(0, 0, True, first=True)
    advance(0, 1, True, first=True)
    for d in range(1, n_wide * 2 // pieces):
        send_x(d)

    def early_step(t, carry):
        both(t, True)
        return spread(t, carry)

    def late_step(t, carry):
        both(t, False)
        return carry

    lax.fori_loop(1, pieces // 2, early_step, 0)
    lax.fori_loop(pieces // 2, pieces - 1, late_step, 0)
    both(pieces - 1, False, last=True)

    def total_of(buf, send, recv, count):
        return copy(buf.at[pl.ds(0, count)], buf.at[pl.ds(0, count)], send, recv, {"row": near})

    load_x.wait()
    others = n_wide - 1
    other_x = copy(x_ref.at[pl.ds(0, others)], xs.at[:, pl.ds(0, others)], send_sem.at[2], x_sem, {"row": near})
    other_x.wait_recv()
    x_rows = xs.shape[1] * xs.shape[2]
    all_done = total_of(vs, send_sem.at[5], done_sem, side)
    all_done.wait_recv()

    def slab(k):
        halves = [vs[h * side + k * HALF:h * side + (k + 1) * HALF].reshape(HALF * BW, SLAB) for h in range(2)]
        return jnp.concatenate(halves, axis=0)

    acc = None
    for k in range(slabs):
        v = slab(k)
        x = xs[k].reshape(x_rows, SLAB)
        product = dot_t(jnp.concatenate([x, v], axis=0), v)
        acc = product if acc is None else acc + product

    wide = 2 * SLAB
    padded = jnp.concatenate([acc, jnp.zeros((acc.shape[0], wide - acc.shape[1]), jnp.float32)], axis=1)
    first_gram = x_rows // 8
    for peer in range(n_wide):
        i, c = peer // 2, peer % 2
        part[peer, 0] = padded[i * 8:(i + 1) * 8, c * SLAB:(c + 1) * SLAB]
        i, c = GRAM_TILES[peer]
        i = i + first_gram
        part[peer, 1] = padded[i * 8:(i + 1) * 8, c * SLAB:(c + 1) * SLAB]

    def scatter(d, carry):
        peer = lax.rem(w + d, n_wide)
        copy(part.at[peer], gather_in.at[w], send_sem.at[3], red_sem, {"wide": peer}).start()
        return carry

    lax.fori_loop(1, n_wide, scatter, 0)
    gather_in[w] = part[w]
    parts_in = total_of(gather_in, send_sem.at[3], red_sem, others)
    parts_in.wait_recv()
    total[...] = jnp.sum(gather_in[...], axis=0)

    def share(d, carry):
        peer = lax.rem(w + d, n_wide)
        copy(total, gathered.at[w], send_sem.at[4], all_sem, {"wide": peer}).start()
        return carry

    lax.fori_loop(1, n_wide, share, 0)
    gathered[w] = total[...]
    totals_in = total_of(gathered, send_sem.at[4], all_sem, others)
    totals_in.wait_recv()

    solved = []
    for c in range(2):
        rows = [gathered[2 * i + c, 0] for i in range(n_wide // 2)]
        rows += [gathered[i, 1] for i in range(n_wide) if GRAM_TILES[i][1] == c]
        solved.append(dot_t(jnp.concatenate(rows, axis=0), diag[c]))
    scaled = []
    for s in range(STEPS):
        c, at = s * BW // SLAB, s * BW % SLAB
        value = solved[c][:x_rows, at:at + BW]
        if s:
            value = value - dot(jnp.concatenate(scaled, axis=1), solved[c][x_rows:x_rows + s * BW, at:at + BW])
        scaled.append(value)
    u = jnp.concatenate(scaled, axis=1)
    for k in range(0, slabs, 2):
        v = jnp.concatenate([slab(k), slab(k + 1)], axis=1)
        x = jnp.concatenate([xs[k].reshape(x_rows, SLAB), xs[k + 1].reshape(x_rows, SLAB)], axis=1)
        out_ref[:, k * SLAB:(k + 2) * SLAB] = x - dot(u, v)

    total_of(own, send_sem.at[0], feed_sem.at[0], side).wait_send()
    copy(flow.at[:, pl.ds(0, side - HALF)], flow.at[:, pl.ds(0, side - HALF)], send_sem.at[1], feed_sem.at[0],
         {"row": near}).wait_send()
    other_x.wait_send()
    all_done.wait_send()
    parts_in.wait_send()
    totals_in.wait_send()


def body(n_row, n_wide, eigvec_t, householder, wy_factor, block_place, offsets):
    local = eigvec_t.shape[0]
    ncols = householder.shape[2]
    slabs = ncols // SLAB
    side = slabs * HALF
    x = eigvec_t.reshape(local, n_wide, slabs, SLAB).transpose(1, 2, 0, 3)
    smem = pl.BlockSpec(memory_space=pltpu.SMEM)
    hbm = pl.BlockSpec(memory_space=pl.ANY)
    f32 = jnp.float32
    return pl.pallas_call(
        functools.partial(kernel, n_row, n_wide),
        out_shape=jax.ShapeDtypeStruct((local * n_wide, ncols), f32),
        in_specs=[smem, smem, hbm, hbm, hbm],
        out_specs=pl.BlockSpec(memory_space=pltpu.VMEM),
        scratch_shapes=[
            pltpu.VMEM(householder.shape, f32),
            pltpu.VMEM(wy_factor.shape, f32),
            pltpu.VMEM((2, SLAB, SLAB), f32),
            pltpu.VMEM((2 * side, BW, SLAB), f32),
            pltpu.VMEM((side, BW, SLAB), f32),
            pltpu.VMEM((2, side, BW, SLAB), f32),
            pltpu.VMEM((2 * side, BW, SLAB), f32),
            pltpu.VMEM((slabs, n_wide, local, SLAB), f32),
            pltpu.VMEM((n_wide, 2, 8, SLAB), f32),
            pltpu.VMEM((n_wide, 2, 8, SLAB), f32),
            pltpu.VMEM((2, 8, SLAB), f32),
            pltpu.VMEM((n_wide, 2, 8, SLAB), f32),
            pltpu.SemaphoreType.DMA((side,)),
            pltpu.SemaphoreType.DMA((2, side)),
            pltpu.SemaphoreType.DMA,
            pltpu.SemaphoreType.DMA,
            pltpu.SemaphoreType.DMA,
            pltpu.SemaphoreType.DMA,
            pltpu.SemaphoreType.DMA((6,)),
            pltpu.SemaphoreType.DMA((3,)),
        ],
        compiler_params=pltpu.CompilerParams(collective_id=0, has_side_effects=True, vmem_limit_bytes=60 << 20),
    )(block_place, offsets, x, householder, wy_factor)


def solution(mesh):
    n_row, n_wide = mesh.shape["row"], mesh.shape["wide"]
    return jax.shard_map(
        functools.partial(body, n_row, n_wide),
        mesh=mesh,
        in_specs=(P(("row", "wide"), None), P("row", None, "wide"), P(), P(), P()),
        out_specs=P("row", "wide"),
        check_vma=False,
    )
```

time: 90 us -> 75.7 us (0.84)
  Pallas kernels: 85.3 us -> 73.7 us
  local copies, waits for them, and re-layouts: 4.44 us -> 1.89 us
    pallas_call x1, Pallas kernels: 85.3 us -> 73.7 us  [body(): pl.pallas_call(functools.partial(kernel, n_row, n_wide), out_shape=jax.Sh...]
    unnamed x11 -> x1, local copies, waits for them, and re-layouts: 4.44 us -> 1.89 us
where the time goes in v3:
time: 75.7 us; the launch traced here: 75.5 us
  Pallas kernels  73.7 us (97%)
  local copies, waits for them, and re-layouts  1.89 us (2%)
    pallas_call x1, Pallas kernels, body(): pl.pallas_call(functools.partial(kernel, n_row, n_wide), out_shape=jax.Sh...  73.7 us
    unnamed x1, local copies, waits for them, and re-layouts  1.89 us

profile of v3, /device:TPU:1, one launch (start us, length us, event | category | flops | bytes accessed | tf_op | source)
XLA Modules:
  0.0 75.5 jit_solution(3573061852236383192)
XLA Ops:
  0.0 73.7 %shard_map.55 = f32[128,1024]{1,0:T(8,128)} custom-call(s32[6]{0:T(128)} %place_ref.1, s32[6]{0:T(128)} %offset_ref.1, f32[32,8,4,128]{3,2,1,0:T(4,128)} %bitcast.3, f32[4,32,1024]{2,1,0:T(8,128)} %h_hbm.1, f32[6,32,32]{2,1,0:T(8,128)} %t_hbm.1), custom_call_target="tpu_custom_call" | custom-call | tf_op jit(solution)/shard_map/pallas_call | solution.py:245
  73.7 1.9 %copy.7 = f32[128,1024]{1,0:T(8,128)} copy(f32[128,1024]{1,0:T(8,128)} %shard_map.55) | data formatting | bytes 1048576

commit v4 on v3

--- a/solution.py
+++ b/solution.py
@@ -22,9 +22,10 @@
     return jnp.dot(a, b, precision=HIGHEST, preferred_element_type=jnp.float32)
 
 
-def kernel(n_row, n_wide, place_ref, offset_ref, x_ref, h_hbm, t_hbm, out_ref,
-           h_ref, t_ref, diag, own, feed, flow, vs, xs, part, gather_in, total, gathered,
-           feed_sem, flow_sem, done_sem, x_sem, red_sem, all_sem, send_sem, local_sem):
+def kernel(n_row, n_wide, place_hbm, offset_hbm, x_ref, h_hbm, t_hbm, out_ref,
+           place_ref, offset_ref, h_ref, t_ref, diag, own, feed, flow, vs, xs,
+           part, core_in, pair, gather_in, total, gathered,
+           feed_sem, flow_sem, done_sem, x_sem, core_sem, red_sem, all_sem, send_sem, local_sem):
     r = lax.axis_index("row")
     w = lax.axis_index("wide")
     slots = h_ref.shape[0]
@@ -52,10 +53,16 @@
     load_h = pltpu.make_async_copy(h_hbm, h_ref, local_sem.at[0])
     load_t = pltpu.make_async_copy(t_hbm, t_ref, local_sem.at[1])
     load_x = pltpu.make_async_copy(x_ref.at[w], xs.at[:, w], local_sem.at[2])
+    load_place = pltpu.make_async_copy(place_hbm, place_ref, local_sem.at[3])
+    load_offset = pltpu.make_async_copy(offset_hbm, offset_ref, local_sem.at[4])
+    load_place.start()
+    load_offset.start()
     load_h.start()
     load_t.start()
     load_x.start()
     lax.fori_loop(1, n_wide, greet, 0)
+    load_place.wait()
+    load_offset.wait()
     load_h.wait()
 
     lane = lax.broadcasted_iota(jnp.int32, (BW, SLAB), 1) + w * (slabs * SLAB)
@@ -65,7 +72,7 @@
         slot = lax.rem(place, slots)
         for k in range(slabs):
             block = h_ref[slot, :, k * SLAB:(k + 1) * SLAB]
-            own[(s // HALF) * side + k * HALF + s % HALF] = jnp.where(lane + k * SLAB >= start, block, 0.0)
+            own[k * STEPS + s] = jnp.where(lane + k * SLAB >= start, block, 0.0)
 
     load_t.wait()
     diag[...] = jnp.zeros_like(diag)
@@ -162,54 +169,70 @@
     other_x.wait_recv()
     x_rows = xs.shape[1] * xs.shape[2]
     all_done = total_of(vs, send_sem.at[5], done_sem, side)
+
+    def slab(k):
+        return vs[pl.ds(k * STEPS, STEPS)].reshape(STEPS * BW, SLAB)
+
+    def products(first):
+        acc = None
+        for m in range(slabs // 2):
+            v = slab(first + m)
+            x = xs[first + m].reshape(x_rows, SLAB)
+            product = dot_t(jnp.concatenate([x, v], axis=0), v)
+            acc = product if acc is None else acc + product
+        return acc
+
+    acc = products(q * (slabs // 2))
     all_done.wait_recv()
-
-    def slab(k):
-        halves = [vs[h * side + k * HALF:h * side + (k + 1) * HALF].reshape(HALF * BW, SLAB) for h in range(2)]
-        return jnp.concatenate(halves, axis=0)
-
-    acc = None
-    for k in range(slabs):
-        v = slab(k)
-        x = xs[k].reshape(x_rows, SLAB)
-        product = dot_t(jnp.concatenate([x, v], axis=0), v)
-        acc = product if acc is None else acc + product
+    acc = acc + products((1 - q) * (slabs // 2))
 
     wide = 2 * SLAB
     padded = jnp.concatenate([acc, jnp.zeros((acc.shape[0], wide - acc.shape[1]), jnp.float32)], axis=1)
     first_gram = x_rows // 8
-    for peer in range(n_wide):
-        i, c = peer // 2, peer % 2
-        part[peer, 0] = padded[i * 8:(i + 1) * 8, c * SLAB:(c + 1) * SLAB]
-        i, c = GRAM_TILES[peer]
-        i = i + first_gram
-        part[peer, 1] = padded[i * 8:(i + 1) * 8, c * SLAB:(c + 1) * SLAB]
-
-    def scatter(d, carry):
-        peer = lax.rem(w + d, n_wide)
-        copy(part.at[peer], gather_in.at[w], send_sem.at[3], red_sem, {"wide": peer}).start()
-        return carry
-
-    lax.fori_loop(1, n_wide, scatter, 0)
-    gather_in[w] = part[w]
-    parts_in = total_of(gather_in, send_sem.at[3], red_sem, others)
+    core = lax.rem(w, 2)
+    chip = lax.div(w, 2)
+    twin = w + 1 - 2 * core
+    chips = n_wide // 2
+    for i in range(chips):
+        for c in range(2):
+            part[c, i, 0] = padded[i * 8:(i + 1) * 8, c * SLAB:(c + 1) * SLAB]
+            tile, column = GRAM_TILES[2 * i + c]
+            tile = tile + first_gram
+            part[c, i, 1] = padded[tile * 8:(tile + 1) * 8, column * SLAB:(column + 1) * SLAB]
+
+    to_twin = copy(part.at[1 - core], core_in, send_sem.at[6], core_sem.at[0], {"wide": twin})
+    to_twin.start()
+    to_twin.wait_recv()
+    pair[...] = part[core] + core_in[...]
+
+    around = sorted(((dx, dy) for dx in range(4) for dy in range(4) if dx or dy),
+                    key=lambda at: -min(at[0], 4 - at[0]) - min(at[1], 4 - at[1]))
+
+    def chip_at(dx, dy):
+        return lax.rem(lax.div(chip, 4) + dx, 4) * 4 + lax.rem(lax.rem(chip, 4) + dy, 4)
+
+    for dx, dy in around:
+        to = chip_at(dx, dy)
+        copy(pair.at[to], gather_in.at[chip], send_sem.at[3], red_sem, {"wide": 2 * to + core}).start()
+    gather_in[chip] = pair[chip]
+    parts_in = total_of(gather_in, send_sem.at[3], red_sem, chips - 1)
     parts_in.wait_recv()
     total[...] = jnp.sum(gather_in[...], axis=0)
 
-    def share(d, carry):
-        peer = lax.rem(w + d, n_wide)
-        copy(total, gathered.at[w], send_sem.at[4], all_sem, {"wide": peer}).start()
-        return carry
-
-    lax.fori_loop(1, n_wide, share, 0)
-    gathered[w] = total[...]
-    totals_in = total_of(gathered, send_sem.at[4], all_sem, others)
+    for dx, dy in around:
+        to = chip_at(dx, dy)
+        copy(total, gathered.at[core, chip], send_sem.at[4], all_sem, {"wide": 2 * to + core}).start()
+    gathered[core, chip] = total[...]
+    totals_in = total_of(gather_in, send_sem.at[4], all_sem, chips - 1)
     totals_in.wait_recv()
+    all_to_twin = copy(gathered.at[core], gathered.at[core], send_sem.at[7], core_sem.at[1], {"wide": twin})
+    all_to_twin.start()
+    all_to_twin.wait_recv()
 
     solved = []
     for c in range(2):
-        rows = [gathered[2 * i + c, 0] for i in range(n_wide // 2)]
-        rows += [gathered[i, 1] for i in range(n_wide) if GRAM_TILES[i][1] == c]
+        rows = [gathered[c, i, 0] for i in range(chips)]
+        rows += [gathered[i % 2, i // 2, 1] for i in range(n_wide) if GRAM_TILES[i][1] == c]
         solved.append(dot_t(jnp.concatenate(rows, axis=0), diag[c]))
     scaled = []
     for s in range(STEPS):
@@ -231,6 +254,8 @@
     all_done.wait_send()
     parts_in.wait_send()
     totals_in.wait_send()
+    to_twin.wait_send()
+    all_to_twin.wait_send()
 
 
 def body(n_row, n_wide, eigvec_t, householder, wy_factor, block_place, offsets):
@@ -239,15 +264,19 @@
     slabs = ncols // SLAB
     side = slabs * HALF
     x = eigvec_t.reshape(local, n_wide, slabs, SLAB).transpose(1, 2, 0, 3)
-    smem = pl.BlockSpec(memory_space=pltpu.SMEM)
-    hbm = pl.BlockSpec(memory_space=pl.ANY)
+    chips = n_wide // 2
+    hbm = pl.BlockSpec(memory_space=pltpu.HBM)
+    operands = [pltpu.with_memory_space_constraint(v, pltpu.HBM)
+                for v in (block_place, offsets, x, householder, wy_factor)]
     f32 = jnp.float32
     return pl.pallas_call(
         functools.partial(kernel, n_row, n_wide),
         out_shape=jax.ShapeDtypeStruct((local * n_wide, ncols), f32),
-        in_specs=[smem, smem, hbm, hbm, hbm],
+        in_specs=[hbm] * 5,
         out_specs=pl.BlockSpec(memory_space=pltpu.VMEM),
         scratch_shapes=[
+            pltpu.SMEM(block_place.shape, jnp.int32),
+            pltpu.SMEM(offsets.shape, jnp.int32),
             pltpu.VMEM(householder.shape, f32),
             pltpu.VMEM(wy_factor.shape, f32),
             pltpu.VMEM((2, SLAB, SLAB), f32),
@@ -256,21 +285,24 @@
             pltpu.VMEM((2, side, BW, SLAB), f32),
             pltpu.VMEM((2 * side, BW, SLAB), f32),
             pltpu.VMEM((slabs, n_wide, local, SLAB), f32),
-            pltpu.VMEM((n_wide, 2, 8, SLAB), f32),
-            pltpu.VMEM((n_wide, 2, 8, SLAB), f32),
+            pltpu.VMEM((2, chips, 2, 8, SLAB), f32),
+            pltpu.VMEM((chips, 2, 8, SLAB), f32),
+            pltpu.VMEM((chips, 2, 8, SLAB), f32),
+            pltpu.VMEM((chips, 2, 8, SLAB), f32),
             pltpu.VMEM((2, 8, SLAB), f32),
-            pltpu.VMEM((n_wide, 2, 8, SLAB), f32),
+            pltpu.VMEM((2, chips, 2, 8, SLAB), f32),
             pltpu.SemaphoreType.DMA((side,)),
             pltpu.SemaphoreType.DMA((2, side)),
             pltpu.SemaphoreType.DMA,
             pltpu.SemaphoreType.DMA,
+            pltpu.SemaphoreType.DMA((2,)),
             pltpu.SemaphoreType.DMA,
             pltpu.SemaphoreType.DMA,
-            pltpu.SemaphoreType.DMA((6,)),
-            pltpu.SemaphoreType.DMA((3,)),
+            pltpu.SemaphoreType.DMA((8,)),
+            pltpu.SemaphoreType.DMA((5,)),
         ],
-        compiler_params=pltpu.CompilerParams(collective_id=0, has_side_effects=True, vmem_limit_bytes=60 << 20),
-    )(block_place, offsets, x, householder, wy_factor)
+        compiler_params=pltpu.CompilerParams(collective_id=0, has_side_effects=True, vmem_limit_bytes=32 << 20),
+    )(*operands)
 
 
 def solution(mesh):

time: 75.7 us -> 71.3 us (0.942)
  Pallas kernels: 73.7 us -> 70.4 us
  local copies, waits for them, and re-layouts: 1.89 us -> 0.8 us
    pallas_call x1, Pallas kernels: 73.7 us -> 70.4 us  [body(): pl.pallas_call(functools.partial(kernel, n_row, n_wide), out_shape=jax.Sh...]
    unnamed x1, local copies, waits for them, and re-layouts: 1.89 us -> 0.8 us
where the time goes in v4:
time: 71.3 us; the launch traced here: 71.2 us
  Pallas kernels  70.4 us (99%)
  local copies, waits for them, and re-layouts  0.8 us (1%)
    pallas_call x1, Pallas kernels, body(): pl.pallas_call(functools.partial(kernel, n_row, n_wide), out_shape=jax.Sh...  70.4 us

profile of v4, /device:TPU:1, one launch (start us, length us, event | category | flops | bytes accessed | tf_op | source)
XLA Modules:
  0.0 71.2 jit_solution(3931522167298391595)
XLA Ops:
  0.0 70.4 %shard_map.55 = f32[128,1024]{1,0:T(8,128)S(1)} custom-call(s32[6]{0:T(128)} %place_hbm.1, s32[6]{0:T(128)} %offset_hbm.1, f32[32,8,4,128]{3,2,1,0:T(4,128)} %bitcast.3, f32[4,32,1024]{2,1,0:T(8,128)} %h_hbm.1, f32[6,32,32]{2,1,0:T(8,128)} %t_hbm.1), custom_call_target="tpu_custom_call" | custom-call | tf_op jit(solution)/shard_map/pallas_call | solution.py:272
  70.4 0.8 %copy.7 = f32[128,1024]{1,0:T(8,128)} copy(f32[128,1024]{1,0:T(8,128)S(1)} %shard_map.55) | data formatting | bytes 1048576

commit v5 on v4

--- a/solution.py
+++ b/solution.py
@@ -10,7 +10,9 @@
 HIGHEST = lax.Precision.HIGHEST
 MESH = pl.DeviceIdType.MESH
 STEPS, BW, SLAB, CUBE = 6, 32, 128, 4
-HALF = STEPS // 2
+PIECE = STEPS // 2 * BW
+CUTS = 3
+CHUNK = PIECE // CUTS
 GRAM_TILES = [(i, 0) for i in range(12)] + [(i, 1) for i in range(20)]
 
 
@@ -31,7 +33,7 @@
     slots = h_ref.shape[0]
     slabs = h_ref.shape[2] // SLAB
     pieces = slabs
-    side = pieces * HALF
+    side = pieces * PIECE
     q = lax.rem(r, 2)
     a = lax.div(r, 2)
     mine, other = q * side, (1 - q) * side
@@ -72,97 +74,115 @@
         slot = lax.rem(place, slots)
         for k in range(slabs):
             block = h_ref[slot, :, k * SLAB:(k + 1) * SLAB]
-            own[k * STEPS + s] = jnp.where(lane + k * SLAB >= start, block, 0.0)
+            own[pl.ds((k * STEPS + s) * BW, BW)] = jnp.where(lane + k * SLAB >= start, block, 0.0)
+
+    pl.semaphore_wait(barrier, n_wide + 3)
+
+    def copy(src, dst, send, recv, to):
+        return pltpu.make_async_remote_copy(
+            src_ref=src, dst_ref=dst, send_sem=send, recv_sem=recv, device_id=to, device_id_type=MESH)
+
+    def span(start, size):
+        return pl.ds(pl.multiple_of(start, 8), size)
+
+    def send_feed(t):
+        for to, odd in ((near, 0), (far, 1)):
+            i = lax.div(to, 2) - t + pieces
+            i = lax.rem(i + lax.rem(i + odd, 2) * (1 + 2 * t), pieces)
+            for at, size, n in chunks_of(i, isinstance(t, int)):
+                copy(own.at[span(other + at, size)], feed.at[span(at, size)], send_sem.at[0], feed_sem.at[n],
+                     {"row": to}).start()
+
+    def chunks_of(i, single):
+        return [(i * PIECE + j * CHUNK, CHUNK, i * CUTS + j) for j in range(CUTS)] if single else [(i * PIECE, PIECE, i * CUTS)]
+
+    def send_x(d):
+        peer = lax.rem(w + d, n_wide)
+        copy(x_ref.at[peer], xs.at[:, w], send_sem.at[2], x_sem, {"wide": peer}).start()
+
+    def hop(t, d, at, j):
+        buf = flow.at[d, span(at, CHUNK)]
+        return copy(buf, buf, send_sem.at[1], flow_sem.at[d, (t + 1) * CUTS + j], {"row": row(2 - 4 * d)})
+
+    def send_finished(t, d, single):
+        i = piece(t, d)
+        to = near + lax.rem(i, 2) * (far - near)
+        for at, size, n in chunks_of(i, single):
+            here, flowed = span(mine + at, size), span(at, size)
+            vs[here] = flow[0, flowed] + flow[1, flowed] - own[here]
+            copy(vs.at[here], vs.at[here], send_sem.at[5], done_sem, {"row": to}).start()
+
+    def piece(t, d):
+        return lax.rem(a - t + d * (1 + 2 * t) + pieces, pieces)
+
+    def add_feed(t, d, single):
+        for at, size, n in chunks_of(piece(t, d), single):
+            here, fed = span(mine + at, size), span(at, size)
+            copy(own.at[here], feed.at[fed], send_sem.at[0], feed_sem.at[n], {"row": near}).wait_recv()
+            own[here] = own[here] + feed[fed]
+
+    def advance(t, d, first=False, last=False):
+        for j in range(CUTS):
+            at = piece(t, d) * PIECE + j * CHUNK
+            here, flowed = span(mine + at, CHUNK), span(at, CHUNK)
+            if first:
+                flow[d, flowed] = own[here]
+            else:
+                hop(t - 1, d, at, j).wait_recv()
+                flow[d, flowed] = flow[d, flowed] + own[here]
+            if not last:
+                hop(t, d, at, j).start()
+
+    def first_stream(t):
+        crossed_right = lax.div(r + 2 * n_row, CUBE) - lax.div(r + 2 * n_row - 2 * t, CUBE)
+        crossed_left = lax.div(r + 2 * t, CUBE) - lax.div(r, CUBE)
+        return lax.div(crossed_right - crossed_left + 1, 2)
+
+    def spread(t):
+        share = n_wide * 2 // pieces
+        lax.fori_loop(t * share, (t + 1) * share, lambda d, c: (send_x(d), c)[1], 0)
+
+    def early_step(t, carry):
+        for d in range(2):
+            add_feed(t, d, False)
+        d = first_stream(t)
+        advance(t, d)
+        advance(t, 1 - d)
+        pl.when(t < pieces // 2 - 2)(lambda: send_feed(t + 2))
+        spread(t)
+        return carry
+
+    def late_step(t, carry):
+        d = first_stream(t)
+        advance(t, d)
+        advance(t, 1 - d)
+        send_finished(t, d, True)
+        send_finished(t, 1 - d, True)
+        return carry
+
+    send_feed(0)
+    send_feed(jnp.int32(1))
+    for d in range(2):
+        add_feed(0, d, True)
+        advance(0, d, first=True)
+    send_feed(jnp.int32(2))
+    for d in range(1, n_wide * 2 // pieces):
+        send_x(d)
+    lax.fori_loop(1, pieces // 2, early_step, 0)
+    lax.fori_loop(pieces // 2, pieces - 1, late_step, 0)
+    d = first_stream(pieces - 1)
+    for d in (d, 1 - d):
+        advance(pieces - 1, d, last=True)
+        send_finished(pieces - 1, d, True)
+
+    def total_of(buf, send, recv, count):
+        return copy(buf.at[pl.ds(0, count)], buf.at[pl.ds(0, count)], send, recv, {"row": near})
 
     load_t.wait()
     diag[...] = jnp.zeros_like(diag)
     for s in range(STEPS):
         at = s * BW % SLAB
         diag[s * BW // SLAB, at:at + BW, at:at + BW] = t_ref[s]
-    pl.semaphore_wait(barrier, n_wide + 3)
-
-    def copy(src, dst, send, recv, to):
-        return pltpu.make_async_remote_copy(
-            src_ref=src, dst_ref=dst, send_sem=send, recv_sem=recv, device_id=to, device_id_type=MESH)
-
-    def send_feed(i, to):
-        for j in range(HALF):
-            c = i * HALF + j
-            copy(own.at[other + c], feed.at[c], send_sem.at[0], feed_sem.at[c], {"row": to}).start()
-
-    for t in range(pieces // 2):
-        i = lax.div(near, 2) - t + pieces
-        send_feed(lax.rem(i + lax.rem(i, 2) * (1 + 2 * t), pieces), near)
-        i = lax.div(far, 2) - t + pieces
-        send_feed(lax.rem(i + (1 - lax.rem(i, 2)) * (1 + 2 * t), pieces), far)
-
-    def send_x(d):
-        peer = lax.rem(w + d, n_wide)
-        copy(x_ref.at[peer], xs.at[:, w], send_sem.at[2], x_sem, {"wide": peer}).start()
-
-    def hop(t, d, c, j):
-        to = row(2 - 4 * d)
-        return copy(flow.at[d, c], flow.at[d, c], send_sem.at[1], flow_sem.at[d, (t + 1) * HALF + j], {"row": to})
-
-    def finished(i, c):
-        sub = lax.rem(i, 2)
-        to = near + sub * (far - near)
-        return copy(vs.at[mine + c], vs.at[mine + c], send_sem.at[5], done_sem, {"row": to})
-
-    def advance(t, d, early, first=False, last=False):
-        i = lax.rem(a - t + d * (1 + 2 * t) + pieces, pieces)
-        for j in range(HALF):
-            c = i * HALF + j
-            if early:
-                copy(own.at[mine + c], feed.at[c], send_sem.at[0], feed_sem.at[c], {"row": near}).wait_recv()
-                base = own[mine + c] + feed[c]
-                own[mine + c] = base
-            else:
-                base = own[mine + c]
-            if first:
-                value = base
-            else:
-                hop(t - 1, d, c, j).wait_recv()
-                value = flow[d, c] + base
-            flow[d, c] = value
-            if not last:
-                hop(t, d, c, j).start()
-            if not early:
-                vs[mine + c] = value + flow[1 - d, c] - base
-                finished(i, c).start()
-
-    def both(t, early, last=False):
-        crossed_right = lax.div(r + 2 * n_row, CUBE) - lax.div(r + 2 * n_row - 2 * t, CUBE)
-        crossed_left = lax.div(r + 2 * t, CUBE) - lax.div(r, CUBE)
-        d = lax.div(crossed_right - crossed_left + 1, 2)
-        advance(t, d, early, last=last)
-        advance(t, 1 - d, early, last=last)
-
-    def spread(t, carry):
-        share = n_wide * 2 // pieces
-        lax.fori_loop(t * share, (t + 1) * share, lambda d, c: (send_x(d), c)[1], 0)
-        return carry
-
-    advance(0, 0, True, first=True)
-    advance(0, 1, True, first=True)
-    for d in range(1, n_wide * 2 // pieces):
-        send_x(d)
-
-    def early_step(t, carry):
-        both(t, True)
-        return spread(t, carry)
-
-    def late_step(t, carry):
-        both(t, False)
-        return carry
-
-    lax.fori_loop(1, pieces // 2, early_step, 0)
-    lax.fori_loop(pieces // 2, pieces - 1, late_step, 0)
-    both(pieces - 1, False, last=True)
-
-    def total_of(buf, send, recv, count):
-        return copy(buf.at[pl.ds(0, count)], buf.at[pl.ds(0, count)], send, recv, {"row": near})
-
     load_x.wait()
     others = n_wide - 1
     other_x = copy(x_ref.at[pl.ds(0, others)], xs.at[:, pl.ds(0, others)], send_sem.at[2], x_sem, {"row": near})
@@ -171,13 +191,18 @@
     all_done = total_of(vs, send_sem.at[5], done_sem, side)
 
     def slab(k):
-        return vs[pl.ds(k * STEPS, STEPS)].reshape(STEPS * BW, SLAB)
+        return vs[span(k * (STEPS * BW), STEPS * BW)]
+
+    def x_slab(k):
+        return xs[k].reshape(x_rows, SLAB)
+
+    def pair_of(part_of, k):
+        return jnp.concatenate([part_of(k), part_of(k + 1)], axis=1)
 
     def products(first):
         acc = None
-        for m in range(slabs // 2):
-            v = slab(first + m)
-            x = xs[first + m].reshape(x_rows, SLAB)
+        for m in range(0, slabs // 2, 2):
+            v, x = pair_of(slab, first + m), pair_of(x_slab, first + m)
             product = dot_t(jnp.concatenate([x, v], axis=0), v)
             acc = product if acc is None else acc + product
         return acc
@@ -243,12 +268,10 @@
         scaled.append(value)
     u = jnp.concatenate(scaled, axis=1)
     for k in range(0, slabs, 2):
-        v = jnp.concatenate([slab(k), slab(k + 1)], axis=1)
-        x = jnp.concatenate([xs[k].reshape(x_rows, SLAB), xs[k + 1].reshape(x_rows, SLAB)], axis=1)
-        out_ref[:, k * SLAB:(k + 2) * SLAB] = x - dot(u, v)
+        out_ref[:, k * SLAB:(k + 2) * SLAB] = pair_of(x_slab, k) - dot(u, pair_of(slab, k))
 
     total_of(own, send_sem.at[0], feed_sem.at[0], side).wait_send()
-    copy(flow.at[:, pl.ds(0, side - HALF)], flow.at[:, pl.ds(0, side - HALF)], send_sem.at[1], feed_sem.at[0],
+    copy(flow.at[:, pl.ds(0, side - PIECE)], flow.at[:, pl.ds(0, side - PIECE)], send_sem.at[1], feed_sem.at[0],
          {"row": near}).wait_send()
     other_x.wait_send()
     all_done.wait_send()
@@ -262,7 +285,7 @@
     local = eigvec_t.shape[0]
     ncols = householder.shape[2]
     slabs = ncols // SLAB
-    side = slabs * HALF
+    side = slabs * PIECE
     x = eigvec_t.reshape(local, n_wide, slabs, SLAB).transpose(1, 2, 0, 3)
     chips = n_wide // 2
     hbm = pl.BlockSpec(memory_space=pltpu.HBM)
@@ -280,10 +303,10 @@
             pltpu.VMEM(householder.shape, f32),
             pltpu.VMEM(wy_factor.shape, f32),
             pltpu.VMEM((2, SLAB, SLAB), f32),
-            pltpu.VMEM((2 * side, BW, SLAB), f32),
-            pltpu.VMEM((side, BW, SLAB), f32),
-            pltpu.VMEM((2, side, BW, SLAB), f32),
-            pltpu.VMEM((2 * side, BW, SLAB), f32),
+            pltpu.VMEM((2 * side, SLAB), f32),
+            pltpu.VMEM((side, SLAB), f32),
+            pltpu.VMEM((2, side, SLAB), f32),
+            pltpu.VMEM((2 * side, SLAB), f32),
             pltpu.VMEM((slabs, n_wide, local, SLAB), f32),
             pltpu.VMEM((2, chips, 2, 8, SLAB), f32),
             pltpu.VMEM((chips, 2, 8, SLAB), f32),
@@ -291,8 +314,8 @@
             pltpu.VMEM((chips, 2, 8, SLAB), f32),
             pltpu.VMEM((2, 8, SLAB), f32),
             pltpu.VMEM((2, chips, 2, 8, SLAB), f32),
-            pltpu.SemaphoreType.DMA((side,)),
-            pltpu.SemaphoreType.DMA((2, side)),
+            pltpu.SemaphoreType.DMA((slabs * CUTS,)),
+            pltpu.SemaphoreType.DMA((2, slabs * CUTS)),
             pltpu.SemaphoreType.DMA,
             pltpu.SemaphoreType.DMA,
             pltpu.SemaphoreType.DMA((2,)),

time: 71.3 us -> 68.8 us (0.965)
  Pallas kernels: 70.4 us -> 67.9 us
    pallas_call x1, Pallas kernels: 70.4 us -> 67.9 us  [body(): pl.pallas_call(functools.partial(kernel, n_row, n_wide), out_shape=jax.Sh...]
where the time goes in v5:
time: 68.8 us; the launch traced here: 68.7 us
  Pallas kernels  67.9 us (99%)
  local copies, waits for them, and re-layouts  0.8 us (1%)
    pallas_call x1, Pallas kernels, body(): pl.pallas_call(functools.partial(kernel, n_row, n_wide), out_shape=jax.Sh...  67.9 us

profile of v5, /device:TPU:1, one launch (start us, length us, event | category | flops | bytes accessed | tf_op | source)
XLA Modules:
  0.0 68.7 jit_solution(3286405363229021391)
XLA Ops:
  0.0 67.9 %shard_map.55 = f32[128,1024]{1,0:T(8,128)S(1)} custom-call(s32[6]{0:T(128)} %place_hbm.1, s32[6]{0:T(128)} %offset_hbm.1, f32[32,8,4,128]{3,2,1,0:T(4,128)} %bitcast.3, f32[4,32,1024]{2,1,0:T(8,128)} %h_hbm.1, f32[6,32,32]{2,1,0:T(8,128)} %t_hbm.1), custom_call_target="tpu_custom_call" | custom-call | tf_op jit(solution)/shard_map/pallas_call | solution.py:295
  67.9 0.8 %copy.7 = f32[128,1024]{1,0:T(8,128)} copy(f32[128,1024]{1,0:T(8,128)S(1)} %shard_map.55) | data formatting | bytes 1048576

commit v6 on v5

--- a/solution.py
+++ b/solution.py
@@ -10,9 +10,11 @@
 HIGHEST = lax.Precision.HIGHEST
 MESH = pl.DeviceIdType.MESH
 STEPS, BW, SLAB, CUBE = 6, 32, 128, 4
-PIECE = STEPS // 2 * BW
-CUTS = 3
-CHUNK = PIECE // CUTS
+FREE = STEPS - 2
+CUTS = FREE // 2
+LINES, LAG = 1, 1
+PIECE = CUTS * BW
+CHUNK = BW
 GRAM_TILES = [(i, 0) for i in range(12)] + [(i, 1) for i in range(20)]
 
 
@@ -25,9 +27,9 @@
 
 
 def kernel(n_row, n_wide, place_hbm, offset_hbm, x_ref, h_hbm, t_hbm, out_ref,
-           place_ref, offset_ref, h_ref, t_ref, diag, own, feed, flow, vs, xs,
+           place_ref, offset_ref, h_ref, t_ref, diag, own, feed, flow, mine_v, other_v, xs,
            part, core_in, pair, gather_in, total, gathered,
-           feed_sem, flow_sem, done_sem, x_sem, core_sem, red_sem, all_sem, send_sem, local_sem):
+           feed_sem, flow_sem, done_sem, fixed_sem, fixed_done_sem, x_sem, core_sem, red_sem, all_sem, send_sem, local_sem):
     r = lax.axis_index("row")
     w = lax.axis_index("wide")
     slots = h_ref.shape[0]
@@ -67,14 +69,37 @@
     load_offset.wait()
     load_h.wait()
 
+    places = [place_ref[s] for s in range(STEPS)]
+    channel, taken = [], 2
+    for place in places:
+        end = jnp.where(place == slots * n_row - 1, 1, taken)
+        channel.append(jnp.where(place == 0, 0, end))
+        taken = taken + jnp.where((place == 0) | (place == slots * n_row - 1), 0, 1)
+
+    def of_channel(c, values):
+        return sum(jnp.where(channel[s] == c, values[s], 0) for s in range(STEPS))
+
+    starts = [offset_ref[s] for s in range(STEPS)]
     lane = lax.broadcasted_iota(jnp.int32, (BW, SLAB), 1) + w * (slabs * SLAB)
-    for s in range(STEPS):
-        place = place_ref[s]
-        start = jnp.where(lax.div(place, slots) == r, offset_ref[s], n_wide * slabs * SLAB)
+    ends = ((0, 0, 0), (1, n_row - 1, slots - 1))
+    half = slabs // 2
+    for c, home, slot in ends:
+        @pl.when(r == home)
+        def _(c=c, slot=slot):
+            start = of_channel(c, starts)
+            for m in range(half):
+                for held, first in ((mine_v, q * half), (other_v, (1 - q) * half)):
+                    at = pl.multiple_of((first + m) * SLAB, SLAB)
+                    block = h_ref[slot, :, pl.ds(at, SLAB)]
+                    held[m, c] = jnp.where(lane + at >= start, block, 0.0)
+
+    for c in range(FREE):
+        place = of_channel(2 + c, places)
+        start = jnp.where(lax.div(place, slots) == r, of_channel(2 + c, starts), n_wide * slabs * SLAB)
         slot = lax.rem(place, slots)
         for k in range(slabs):
             block = h_ref[slot, :, k * SLAB:(k + 1) * SLAB]
-            own[pl.ds((k * STEPS + s) * BW, BW)] = jnp.where(lane + k * SLAB >= start, block, 0.0)
+            own[pl.ds((k * FREE + c) * BW, BW)] = jnp.where(lane + k * SLAB >= start, block, 0.0)
 
     pl.semaphore_wait(barrier, n_wide + 3)
 
@@ -88,10 +113,11 @@
     def send_feed(t):
         for to, odd in ((near, 0), (far, 1)):
             i = lax.div(to, 2) - t + pieces
-            i = lax.rem(i + lax.rem(i + odd, 2) * (1 + 2 * t), pieces)
-            for at, size, n in chunks_of(i, isinstance(t, int)):
-                copy(own.at[span(other + at, size)], feed.at[span(at, size)], send_sem.at[0], feed_sem.at[n],
-                     {"row": to}).start()
+            i = i + lax.rem(i + odd, 2) * (1 + 2 * t)
+            for line in range(LINES):
+                for at, size, n in chunks_of(lax.rem(i + line * (pieces // LINES), pieces), isinstance(t, int) and t == 0):
+                    copy(own.at[span(other + at, size)], feed.at[span(at, size)], send_sem.at[0], feed_sem.at[n],
+                         {"row": to}).start()
 
     def chunks_of(i, single):
         return [(i * PIECE + j * CHUNK, CHUNK, i * CUTS + j) for j in range(CUTS)] if single else [(i * PIECE, PIECE, i * CUTS)]
@@ -100,38 +126,40 @@
         peer = lax.rem(w + d, n_wide)
         copy(x_ref.at[peer], xs.at[:, w], send_sem.at[2], x_sem, {"wide": peer}).start()
 
-    def hop(t, d, at, j):
-        buf = flow.at[d, span(at, CHUNK)]
-        return copy(buf, buf, send_sem.at[1], flow_sem.at[d, (t + 1) * CUTS + j], {"row": row(2 - 4 * d)})
-
-    def send_finished(t, d, single):
-        i = piece(t, d)
+    def hop(t, d, line, at, j):
+        buf = flow.at[d, line, span(at, CHUNK)]
+        return copy(buf, buf, send_sem.at[1], flow_sem.at[d, line, (t + 1) * CUTS + j], {"row": row(2 - 4 * d)})
+
+    def piece(t, d, line):
+        return lax.rem(a - t + d * (1 + 2 * t) + line * (pieces // LINES) + pieces, pieces)
+
+    def send_finished(t, d, line):
+        i = piece(t, d, line)
         to = near + lax.rem(i, 2) * (far - near)
-        for at, size, n in chunks_of(i, single):
-            here, flowed = span(mine + at, size), span(at, size)
-            vs[here] = flow[0, flowed] + flow[1, flowed] - own[here]
-            copy(vs.at[here], vs.at[here], send_sem.at[5], done_sem, {"row": to}).start()
-
-    def piece(t, d):
-        return lax.rem(a - t + d * (1 + 2 * t) + pieces, pieces)
-
-    def add_feed(t, d, single):
-        for at, size, n in chunks_of(piece(t, d), single):
+        m = lax.div(i, 2)
+        for j in range(CUTS):
+            at, c = i * PIECE + j * CHUNK, 2 + lax.rem(i, 2) * CUTS + j
+            here, flowed = span(mine + at, CHUNK), span(at, CHUNK)
+            mine_v[m, c] = flow[0, line, flowed] + flow[1, line, flowed] - own[here]
+            copy(mine_v.at[m, c], other_v.at[m, c], send_sem.at[5], done_sem, {"row": to}).start()
+
+    def add_feed(t, d, line, single):
+        for at, size, n in chunks_of(piece(t, d, line), single):
             here, fed = span(mine + at, size), span(at, size)
             copy(own.at[here], feed.at[fed], send_sem.at[0], feed_sem.at[n], {"row": near}).wait_recv()
             own[here] = own[here] + feed[fed]
 
-    def advance(t, d, first=False, last=False):
+    def advance(t, d, line, first=False, last=False):
         for j in range(CUTS):
-            at = piece(t, d) * PIECE + j * CHUNK
+            at = piece(t, d, line) * PIECE + j * CHUNK
             here, flowed = span(mine + at, CHUNK), span(at, CHUNK)
             if first:
-                flow[d, flowed] = own[here]
+                flow[d, line, flowed] = own[here]
             else:
-                hop(t - 1, d, at, j).wait_recv()
-                flow[d, flowed] = flow[d, flowed] + own[here]
+                hop(t - 1, d, line, at, j).wait_recv()
+                flow[d, line, flowed] = flow[d, line, flowed] + own[here]
             if not last:
-                hop(t, d, at, j).start()
+                hop(t, d, line, at, j).start()
 
     def first_stream(t):
         crossed_right = lax.div(r + 2 * n_row, CUBE) - lax.div(r + 2 * n_row - 2 * t, CUBE)
@@ -142,38 +170,82 @@
         share = n_wide * 2 // pieces
         lax.fori_loop(t * share, (t + 1) * share, lambda d, c: (send_x(d), c)[1], 0)
 
-    def early_step(t, carry):
+    def fixed(c, home, m):
+        root = home // 2
+        ahead, behind = lax.rem(a - root + pieces, pieces), lax.rem(root - a + pieces, pieces)
+        held = mine_v.at[m, c]
+
+        def to(row_at, source, target, sem):
+            return copy(source.at[m, c], target.at[m, c], send_sem.at[8], sem, {"row": row_at})
+
+        start = to(near, other_v, mine_v, fixed_sem.at[c, m])
+        return jnp.minimum(ahead, behind), start, (
+            (ahead < half, to(row(2), mine_v, mine_v, fixed_sem.at[c, m])),
+            (behind < half - 1, to(row(-2), mine_v, mine_v, fixed_sem.at[c, m])),
+            (near != home, to(near, mine_v, other_v, fixed_done_sem.at[c])))
+
+    def start_fixed():
+        for c, home, slot in ends:
+            @pl.when(r == home)
+            def _(c=c, home=home):
+                for m in range(half):
+                    fixed(c, home, m)[1].start()
+
+    def pass_fixed(t):
+        for c, home, slot in ends:
+            root = home // 2
+            distance = jnp.minimum(lax.rem(a - root + pieces, pieces), lax.rem(root - a + pieces, pieces))
+            m = t - LAG - distance
+
+            @pl.when((m >= 0) & (m < half))
+            def _(c=c, home=home, m=m):
+                distance, start, onward = fixed(c, home, m)
+                pl.when(r != home)(start.wait_recv)
+                for wanted, move in onward:
+                    pl.when(wanted)(move.start)
+
+    def step(t, last=False):
+        d = first_stream(t)
+        for d in (d, 1 - d):
+            for line in range(LINES):
+                advance(t, d, line, last=last)
+
+    feeds = half // LINES
+
+    def feed_in(t, single):
         for d in range(2):
-            add_feed(t, d, False)
-        d = first_stream(t)
-        advance(t, d)
-        advance(t, 1 - d)
-        pl.when(t < pieces // 2 - 2)(lambda: send_feed(t + 2))
+            for line in range(LINES):
+                add_feed(t, d, line, single)
+
+    def middle(t, carry):
+        pl.when(t < feeds)(lambda: feed_in(t, False))
+        step(t)
+        pass_fixed(t)
+        pl.when(t < feeds - 2)(lambda: send_feed(t + 2))
         spread(t)
         return carry
 
-    def late_step(t, carry):
-        d = first_stream(t)
-        advance(t, d)
-        advance(t, 1 - d)
-        send_finished(t, d, True)
-        send_finished(t, 1 - d, True)
-        return carry
-
     send_feed(0)
-    send_feed(jnp.int32(1))
+    start_fixed()
+    send_feed(1)
     for d in range(2):
-        add_feed(0, d, True)
-        advance(0, d, first=True)
-    send_feed(jnp.int32(2))
+        for line in range(LINES):
+            add_feed(0, d, line, True)
+            advance(0, d, line, first=True)
+    if feeds > 2:
+        send_feed(2)
     for d in range(1, n_wide * 2 // pieces):
         send_x(d)
-    lax.fori_loop(1, pieces // 2, early_step, 0)
-    lax.fori_loop(pieces // 2, pieces - 1, late_step, 0)
-    d = first_stream(pieces - 1)
-    for d in (d, 1 - d):
-        advance(pieces - 1, d, last=True)
-        send_finished(pieces - 1, d, True)
+    lax.fori_loop(1, half, middle, 0)
+    hops = half + half // LINES - 1
+    for t in range(half, hops + 1):
+        step(t, last=t == hops)
+        for d in range(2):
+            for line in range(LINES):
+                send_finished(t, d, line)
+        pass_fixed(t)
+    for t in range(hops + 1, 2 * half + LAG):
+        pass_fixed(t)
 
     def total_of(buf, send, recv, count):
         return copy(buf.at[pl.ds(0, count)], buf.at[pl.ds(0, count)], send, recv, {"row": near})
@@ -188,28 +260,31 @@
     other_x = copy(x_ref.at[pl.ds(0, others)], xs.at[:, pl.ds(0, others)], send_sem.at[2], x_sem, {"row": near})
     other_x.wait_recv()
     x_rows = xs.shape[1] * xs.shape[2]
-    all_done = total_of(vs, send_sem.at[5], done_sem, side)
-
-    def slab(k):
-        return vs[span(k * (STEPS * BW), STEPS * BW)]
-
-    def x_slab(k):
-        return xs[k].reshape(x_rows, SLAB)
-
-    def pair_of(part_of, k):
-        return jnp.concatenate([part_of(k), part_of(k + 1)], axis=1)
-
-    def products(first):
+    all_done = total_of(own, send_sem.at[5], done_sem, side)
+
+    def pair_v(held, m):
+        return jnp.concatenate(
+            [jnp.concatenate([held[k, channel[s]] for s in range(STEPS)], axis=0) for k in (m, m + 1)], axis=1)
+
+    def pair_x(k):
+        return jnp.concatenate([xs[k].reshape(x_rows, SLAB), xs[k + 1].reshape(x_rows, SLAB)], axis=1)
+
+    sides = ((mine_v, q * half), (other_v, (1 - q) * half))
+
+    def products(held, first):
         acc = None
-        for m in range(0, slabs // 2, 2):
-            v, x = pair_of(slab, first + m), pair_of(x_slab, first + m)
+        for m in range(0, half, 2):
+            v, x = pair_v(held, m), pair_x(first + m)
             product = dot_t(jnp.concatenate([x, v], axis=0), v)
             acc = product if acc is None else acc + product
         return acc
 
-    acc = products(q * (slabs // 2))
+    acc = products(*sides[0])
     all_done.wait_recv()
-    acc = acc + products((1 - q) * (slabs // 2))
+    for c, home, slot in ends:
+        pl.when(r != home)(copy(mine_v.at[:, c], other_v.at[:, c], send_sem.at[8], fixed_done_sem.at[c],
+                                {"row": near}).wait_recv)
+    acc = acc + products(*sides[1])
 
     wide = 2 * SLAB
     padded = jnp.concatenate([acc, jnp.zeros((acc.shape[0], wide - acc.shape[1]), jnp.float32)], axis=1)
@@ -267,12 +342,20 @@
             value = value - dot(jnp.concatenate(scaled, axis=1), solved[c][x_rows:x_rows + s * BW, at:at + BW])
         scaled.append(value)
     u = jnp.concatenate(scaled, axis=1)
-    for k in range(0, slabs, 2):
-        out_ref[:, k * SLAB:(k + 2) * SLAB] = pair_of(x_slab, k) - dot(u, pair_of(slab, k))
+    for held, first in sides:
+        for m in range(0, half, 2):
+            at = pl.multiple_of((first + m) * SLAB, 2 * SLAB)
+            out_ref[:, pl.ds(at, 2 * SLAB)] = pair_x(first + m) - dot(u, pair_v(held, m))
 
     total_of(own, send_sem.at[0], feed_sem.at[0], side).wait_send()
-    copy(flow.at[:, pl.ds(0, side - PIECE)], flow.at[:, pl.ds(0, side - PIECE)], send_sem.at[1], feed_sem.at[0],
-         {"row": near}).wait_send()
+    flowed = flow.at[:, :, pl.ds(0, hops * PIECE)]
+    copy(flowed, flowed, send_sem.at[1], feed_sem.at[0], {"row": near}).wait_send()
+    for c, home, slot in ends:
+        for m in range(half):
+            distance, start, onward = fixed(c, home, m)
+            pl.when(r == home)(start.wait_send)
+            for wanted, move in onward:
+                pl.when(wanted)(move.wait_send)
     other_x.wait_send()
     all_done.wait_send()
     parts_in.wait_send()
@@ -305,8 +388,9 @@
             pltpu.VMEM((2, SLAB, SLAB), f32),
             pltpu.VMEM((2 * side, SLAB), f32),
             pltpu.VMEM((side, SLAB), f32),
-            pltpu.VMEM((2, side, SLAB), f32),
-            pltpu.VMEM((2 * side, SLAB), f32),
+            pltpu.VMEM((2, LINES, side, SLAB), f32),
+            pltpu.VMEM((slabs // 2, STEPS, BW, SLAB), f32),
+            pltpu.VMEM((slabs // 2, STEPS, BW, SLAB), f32),
             pltpu.VMEM((slabs, n_wide, local, SLAB), f32),
             pltpu.VMEM((2, chips, 2, 8, SLAB), f32),
             pltpu.VMEM((chips, 2, 8, SLAB), f32),
@@ -315,13 +399,15 @@
             pltpu.VMEM((2, 8, SLAB), f32),
             pltpu.VMEM((2, chips, 2, 8, SLAB), f32),
             pltpu.SemaphoreType.DMA((slabs * CUTS,)),
-            pltpu.SemaphoreType.DMA((2, slabs * CUTS)),
+            pltpu.SemaphoreType.DMA((2, LINES, slabs * CUTS)),
             pltpu.SemaphoreType.DMA,
+            pltpu.SemaphoreType.DMA((2, slabs // 2)),
+            pltpu.SemaphoreType.DMA((2,)),
             pltpu.SemaphoreType.DMA,
             pltpu.SemaphoreType.DMA((2,)),
             pltpu.SemaphoreType.DMA,
             pltpu.SemaphoreType.DMA,
-            pltpu.SemaphoreType.DMA((8,)),
+            pltpu.SemaphoreType.DMA((9,)),
             pltpu.SemaphoreType.DMA((5,)),
         ],
         compiler_params=pltpu.CompilerParams(collective_id=0, has_side_effects=True, vmem_limit_bytes=32 << 20),

time: 68.8 us -> 66.2 us (0.962)
  Pallas kernels: 67.9 us -> 65.3 us
    pallas_call x1, Pallas kernels: 67.9 us -> 65.3 us  [body(): pl.pallas_call(functools.partial(kernel, n_row, n_wide), out_shape=jax.Sh...]
where the time goes in v6:
time: 66.2 us; the launch traced here: 66.1 us
  Pallas kernels  65.3 us (99%)
  local copies, waits for them, and re-layouts  0.8 us (1%)
    pallas_call x1, Pallas kernels, body(): pl.pallas_call(functools.partial(kernel, n_row, n_wide), out_shape=jax.Sh...  65.3 us

profile of v6, /device:TPU:1, one launch (start us, length us, event | category | flops | bytes accessed | tf_op | source)
XLA Modules:
  0.0 66.1 jit_solution(11310366809359640075)
XLA Ops:
  0.0 65.3 %shard_map.55 = f32[128,1024]{1,0:T(8,128)S(1)} custom-call(s32[6]{0:T(128)} %place_hbm.1, s32[6]{0:T(128)} %offset_hbm.1, f32[32,8,4,128]{3,2,1,0:T(4,128)} %bitcast.3, f32[4,32,1024]{2,1,0:T(8,128)} %h_hbm.1, f32[6,32,32]{2,1,0:T(8,128)} %t_hbm.1), custom_call_target="tpu_custom_call" | custom-call | tf_op jit(solution)/shard_map/pallas_call | solution.py:378
  65.3 0.8 %copy.7 = f32[128,1024]{1,0:T(8,128)} copy(f32[128,1024]{1,0:T(8,128)S(1)} %shard_map.55) | data formatting | bytes 1048576

commit v7 on v6

--- a/solution.py
+++ b/solution.py
@@ -7,23 +7,40 @@
 from jax.experimental.pallas import tpu as pltpu
 from jax.sharding import PartitionSpec as P
 
-HIGHEST = lax.Precision.HIGHEST
 MESH = pl.DeviceIdType.MESH
 STEPS, BW, SLAB, CUBE = 6, 32, 128, 4
 FREE = STEPS - 2
 CUTS = FREE // 2
-LINES, LAG = 1, 1
+LINES, LAG, GROUP = 2, 1, 2
 PIECE = CUTS * BW
 CHUNK = BW
 GRAM_TILES = [(i, 0) for i in range(12)] + [(i, 1) for i in range(20)]
 
 
+def split(a):
+    high = a.astype(jnp.bfloat16)
+    return high, (a - high.astype(jnp.float32)).astype(jnp.bfloat16)
+
+
+def contract(a, b, dims):
+    (a1, a2), (b1, b2) = split(a), split(b)
+
+    def one(x, y):
+        return lax.dot_general(x, y, (dims, ((), ())), preferred_element_type=jnp.float32)
+
+    return one(a1, b1) + (one(a1, b2) + one(a2, b1))
+
+
+def exact(a, b, dims):
+    return lax.dot_general(a, b, (dims, ((), ())), precision=lax.Precision.HIGHEST, preferred_element_type=jnp.float32)
+
+
 def dot_t(a, b):
-    return lax.dot_general(a, b, (((1,), (1,)), ((), ())), precision=HIGHEST, preferred_element_type=jnp.float32)
+    return contract(a, b, ((1,), (1,)))
 
 
 def dot(a, b):
-    return jnp.dot(a, b, precision=HIGHEST, preferred_element_type=jnp.float32)
+    return contract(a, b, ((1,), (0,)))
 
 
 def kernel(n_row, n_wide, place_hbm, offset_hbm, x_ref, h_hbm, t_hbm, out_ref,
@@ -83,24 +100,20 @@
     lane = lax.broadcasted_iota(jnp.int32, (BW, SLAB), 1) + w * (slabs * SLAB)
     ends = ((0, 0, 0), (1, n_row - 1, slots - 1))
     half = slabs // 2
-    for c, home, slot in ends:
-        @pl.when(r == home)
-        def _(c=c, slot=slot):
-            start = of_channel(c, starts)
-            for m in range(half):
-                for held, first in ((mine_v, q * half), (other_v, (1 - q) * half)):
-                    at = pl.multiple_of((first + m) * SLAB, SLAB)
-                    block = h_ref[slot, :, pl.ds(at, SLAB)]
-                    held[m, c] = jnp.where(lane + at >= start, block, 0.0)
-
+    free = []
     for c in range(FREE):
         place = of_channel(2 + c, places)
         start = jnp.where(lax.div(place, slots) == r, of_channel(2 + c, starts), n_wide * slabs * SLAB)
-        slot = lax.rem(place, slots)
-        for k in range(slabs):
-            block = h_ref[slot, :, k * SLAB:(k + 1) * SLAB]
-            own[pl.ds((k * FREE + c) * BW, BW)] = jnp.where(lane + k * SLAB >= start, block, 0.0)
-
+        free.append((lax.rem(place, slots), start))
+
+    def stage(first):
+        for m in range(half):
+            at = pl.multiple_of((first + m) * SLAB, SLAB)
+            for c, (slot, start) in enumerate(free):
+                block = h_ref[slot, :, pl.ds(at, SLAB)]
+                own[pl.ds(((first + m) * FREE + c) * BW, BW)] = jnp.where(lane + at >= start, block, 0.0)
+
+    stage((1 - q) * half)
     pl.semaphore_wait(barrier, n_wide + 3)
 
     def copy(src, dst, send, recv, to):
@@ -195,14 +208,15 @@
         for c, home, slot in ends:
             root = home // 2
             distance = jnp.minimum(lax.rem(a - root + pieces, pieces), lax.rem(root - a + pieces, pieces))
-            m = t - LAG - distance
-
-            @pl.when((m >= 0) & (m < half))
-            def _(c=c, home=home, m=m):
-                distance, start, onward = fixed(c, home, m)
-                pl.when(r != home)(start.wait_recv)
-                for wanted, move in onward:
-                    pl.when(wanted)(move.start)
+            turn = t - LAG - distance
+
+            @pl.when((turn >= 0) & (turn < half // GROUP))
+            def _(c=c, home=home, turn=turn):
+                for m in range(GROUP):
+                    distance, start, onward = fixed(c, home, turn * GROUP + m)
+                    pl.when(r != home)(start.wait_recv)
+                    for wanted, move in onward:
+                        pl.when(wanted)(move.start)
 
     def step(t, last=False):
         d = first_stream(t)
@@ -226,8 +240,18 @@
         return carry
 
     send_feed(0)
+    for c, home, slot in ends:
+        @pl.when(r == home)
+        def _(c=c, slot=slot):
+            start = of_channel(c, starts)
+            for m in range(half):
+                for held, first in ((mine_v, q * half), (other_v, (1 - q) * half)):
+                    at = pl.multiple_of((first + m) * SLAB, SLAB)
+                    block = h_ref[slot, :, pl.ds(at, SLAB)]
+                    held[m, c] = jnp.where(lane + at >= start, block, 0.0)
     start_fixed()
     send_feed(1)
+    stage(q * half)
     for d in range(2):
         for line in range(LINES):
             add_feed(0, d, line, True)
@@ -244,7 +268,7 @@
             for line in range(LINES):
                 send_finished(t, d, line)
         pass_fixed(t)
-    for t in range(hops + 1, 2 * half + LAG):
+    for t in range(hops + 1, half + half // GROUP + LAG):
         pass_fixed(t)
 
     def total_of(buf, send, recv, count):
@@ -333,13 +357,14 @@
     for c in range(2):
         rows = [gathered[c, i, 0] for i in range(chips)]
         rows += [gathered[i % 2, i // 2, 1] for i in range(n_wide) if GRAM_TILES[i][1] == c]
-        solved.append(dot_t(jnp.concatenate(rows, axis=0), diag[c]))
+        solved.append(exact(jnp.concatenate(rows, axis=0), diag[c], ((1,), (1,))))
     scaled = []
     for s in range(STEPS):
         c, at = s * BW // SLAB, s * BW % SLAB
         value = solved[c][:x_rows, at:at + BW]
         if s:
-            value = value - dot(jnp.concatenate(scaled, axis=1), solved[c][x_rows:x_rows + s * BW, at:at + BW])
+            overlap = solved[c][x_rows:x_rows + s * BW, at:at + BW]
+            value = value - exact(jnp.concatenate(scaled, axis=1), overlap, ((1,), (0,)))
         scaled.append(value)
     u = jnp.concatenate(scaled, axis=1)
     for held, first in sides:

time: 66.2 us -> 63.6 us (0.961)
  Pallas kernels: 65.3 us -> 62.6 us
    pallas_call x1, Pallas kernels: 65.3 us -> 62.6 us  [body(): pl.pallas_call(functools.partial(kernel, n_row, n_wide), out_shape=jax.Sh...]
where the time goes in v7:
time: 63.6 us; the launch traced here: 63.4 us
  Pallas kernels  62.6 us (98%)
  local copies, waits for them, and re-layouts  0.8 us (1%)
    pallas_call x1, Pallas kernels, body(): pl.pallas_call(functools.partial(kernel, n_row, n_wide), out_shape=jax.Sh...  62.6 us

profile of v7, /device:TPU:1, one launch (start us, length us, event | category | flops | bytes accessed | tf_op | source)
XLA Modules:
  0.0 63.4 jit_solution(8174788068835361549)
XLA Ops:
  0.0 62.6 %shard_map.55 = f32[128,1024]{1,0:T(8,128)S(1)} custom-call(s32[6]{0:T(128)} %place_hbm.1, s32[6]{0:T(128)} %offset_hbm.1, f32[32,8,4,128]{3,2,1,0:T(4,128)} %bitcast.3, f32[4,32,1024]{2,1,0:T(8,128)} %h_hbm.1, f32[6,32,32]{2,1,0:T(8,128)} %t_hbm.1), custom_call_target="tpu_custom_call" | custom-call | tf_op jit(solution)/shard_map/pallas_call | solution.py:403
  62.6 0.8 %copy.7 = f32[128,1024]{1,0:T(8,128)} copy(f32[128,1024]{1,0:T(8,128)S(1)} %shard_map.55) | data formatting | bytes 1048576

commit v8 on v7

--- a/solution.py
+++ b/solution.py
@@ -23,16 +23,12 @@
 
 
 def contract(a, b, dims):
-    (a1, a2), (b1, b2) = split(a), split(b)
+    (a1, a2), (b1, b2) = a, b
 
     def one(x, y):
         return lax.dot_general(x, y, (dims, ((), ())), preferred_element_type=jnp.float32)
 
     return one(a1, b1) + (one(a1, b2) + one(a2, b1))
-
-
-def exact(a, b, dims):
-    return lax.dot_general(a, b, (dims, ((), ())), precision=lax.Precision.HIGHEST, preferred_element_type=jnp.float32)
 
 
 def dot_t(a, b):
@@ -220,9 +216,9 @@
 
     def step(t, last=False):
         d = first_stream(t)
-        for d in (d, 1 - d):
-            for line in range(LINES):
-                advance(t, d, line, last=last)
+        for line in range(LINES):
+            for way in (d, 1 - d):
+                advance(t, way, line, last=last)
 
     feeds = half // LINES
 
@@ -264,8 +260,8 @@
     hops = half + half // LINES - 1
     for t in range(half, hops + 1):
         step(t, last=t == hops)
-        for d in range(2):
-            for line in range(LINES):
+        for line in range(LINES):
+            for d in range(2):
                 send_finished(t, d, line)
         pass_fixed(t)
     for t in range(hops + 1, half + half // GROUP + LAG):
@@ -299,7 +295,8 @@
         acc = None
         for m in range(0, half, 2):
             v, x = pair_v(held, m), pair_x(first + m)
-            product = dot_t(jnp.concatenate([x, v], axis=0), v)
+            v, x = split(v), split(x)
+            product = dot_t([jnp.concatenate(both, axis=0) for both in zip(x, v)], v)
             acc = product if acc is None else acc + product
         return acc
 
@@ -357,20 +354,20 @@
     for c in range(2):
         rows = [gathered[c, i, 0] for i in range(chips)]
         rows += [gathered[i % 2, i // 2, 1] for i in range(n_wide) if GRAM_TILES[i][1] == c]
-        solved.append(exact(jnp.concatenate(rows, axis=0), diag[c], ((1,), (1,))))
+        solved.append(dot_t(split(jnp.concatenate(rows, axis=0)), split(diag[c])))
     scaled = []
     for s in range(STEPS):
         c, at = s * BW // SLAB, s * BW % SLAB
         value = solved[c][:x_rows, at:at + BW]
         if s:
             overlap = solved[c][x_rows:x_rows + s * BW, at:at + BW]
-            value = value - exact(jnp.concatenate(scaled, axis=1), overlap, ((1,), (0,)))
+            value = value - dot(split(jnp.concatenate(scaled, axis=1)), split(overlap))
         scaled.append(value)
-    u = jnp.concatenate(scaled, axis=1)
+    u = split(jnp.concatenate(scaled, axis=1))
     for held, first in sides:
         for m in range(0, half, 2):
             at = pl.multiple_of((first + m) * SLAB, 2 * SLAB)
-            out_ref[:, pl.ds(at, 2 * SLAB)] = pair_x(first + m) - dot(u, pair_v(held, m))
+            out_ref[:, pl.ds(at, 2 * SLAB)] = pair_x(first + m) - dot(u, split(pair_v(held, m)))
 
     total_of(own, send_sem.at[0], feed_sem.at[0], side).wait_send()
     flowed = flow.at[:, :, pl.ds(0, hops * PIECE)]

time: 63.6 us -> 62.8 us (0.987)
  Pallas kernels: 62.6 us -> 61.9 us
    pallas_call x1, Pallas kernels: 62.6 us -> 61.9 us  [body(): pl.pallas_call(functools.partial(kernel, n_row, n_wide), out_shape=jax.Sh...]
where the time goes in v8:
time: 62.8 us; the launch traced here: 62.7 us
  Pallas kernels  61.9 us (99%)
  local copies, waits for them, and re-layouts  0.8 us (1%)
    pallas_call x1, Pallas kernels, body(): pl.pallas_call(functools.partial(kernel, n_row, n_wide), out_shape=jax.Sh...  61.9 us

profile of v8, /device:TPU:1, one launch (start us, length us, event | category | flops | bytes accessed | tf_op | source)
XLA Modules:
  0.0 62.7 jit_solution(3785725036200132197)
XLA Ops:
  0.0 61.9 %shard_map.55 = f32[128,1024]{1,0:T(8,128)S(1)} custom-call(s32[6]{0:T(128)} %place_hbm.1, s32[6]{0:T(128)} %offset_hbm.1, f32[32,8,4,128]{3,2,1,0:T(4,128)} %bitcast.3, f32[4,32,1024]{2,1,0:T(8,128)} %h_hbm.1, f32[6,32,32]{2,1,0:T(8,128)} %t_hbm.1), custom_call_target="tpu_custom_call" | custom-call | tf_op jit(solution)/shard_map/pallas_call | solution.py:400
  61.9 0.8 %copy.7 = f32[128,1024]{1,0:T(8,128)} copy(f32[128,1024]{1,0:T(8,128)S(1)} %shard_map.55) | data formatting | bytes 1048576

commit v9 on v8

--- a/solution.py
+++ b/solution.py
@@ -259,10 +259,17 @@
     lax.fori_loop(1, half, middle, 0)
     hops = half + half // LINES - 1
     for t in range(half, hops + 1):
-        step(t, last=t == hops)
-        for line in range(LINES):
-            for d in range(2):
-                send_finished(t, d, line)
+        if t == hops:
+            first = first_stream(t)
+            for line in range(LINES):
+                for d in (first, 1 - first):
+                    advance(t, d, line, last=True)
+                    send_finished(t, d, line)
+        else:
+            step(t)
+            for line in range(LINES):
+                for d in range(2):
+                    send_finished(t, d, line)
         pass_fixed(t)
     for t in range(hops + 1, half + half // GROUP + LAG):
         pass_fixed(t)

time: 62.8 us -> 62.5 us (level)
  no operation moved by 1% of the time
where the time goes in v9:
time: 62.5 us; the launch traced here: 62.3 us
  Pallas kernels  61.5 us (98%)
  local copies, waits for them, and re-layouts  0.8 us (1%)
    pallas_call x1, Pallas kernels, body(): pl.pallas_call(functools.partial(kernel, n_row, n_wide), out_shape=jax.Sh...  61.5 us

profile of v9, /device:TPU:1, one launch (start us, length us, event | category | flops | bytes accessed | tf_op | source)
XLA Modules:
  0.0 62.3 jit_solution(1258914139268366268)
XLA Ops:
  0.0 61.5 %shard_map.55 = f32[128,1024]{1,0:T(8,128)S(1)} custom-call(s32[6]{0:T(128)} %place_hbm.1, s32[6]{0:T(128)} %offset_hbm.1, f32[32,8,4,128]{3,2,1,0:T(4,128)} %bitcast.3, f32[4,32,1024]{2,1,0:T(8,128)} %h_hbm.1, f32[6,32,32]{2,1,0:T(8,128)} %t_hbm.1), custom_call_target="tpu_custom_call" | custom-call | tf_op jit(solution)/shard_map/pallas_call | solution.py:407
  61.5 0.8 %copy.7 = f32[128,1024]{1,0:T(8,128)} copy(f32[128,1024]{1,0:T(8,128)S(1)} %shard_map.55) | data formatting | bytes 1048576
